TPU v7x, 32 devices: a whole 2x2x4 slice. The times are simulated.
32 devices in a mesh: band: 4 (over x, core), grid: 8 (over z, y).
Axes of the slice: x: 2, y: 2, z: 4, core: 2. Of those that a mesh axis runs over, the one named last changes fastest.
Arguments:
- coefficients: bfloat16 [128, 16, 15360], P('grid', None, 'band'), may hold values from -6 to 6
- block_rows: int32 [128], P('grid'), may hold values from 5 to 16
- touch_atoms: int32 [16, 16], P('grid'), may hold values from 0 to 127, as said below
- basis_values: bfloat16 [16, 256, 640], P('grid'), may hold values from -0.375 to 0.375
- outer_field: float32 [16, 640], P('grid'), may hold values from -6 to 6
- occupations: float32 [15360], P('band'), may hold values from 0 to 2
Outputs:
- gradient: float32 [128, 16, 15360], P('grid', None, 'band')
- density: float32 [16, 640], P('grid')
Inputs may be any that keep to these rules, and one draw needn't show every extreme that they name: `touch_atoms`: each row names 16 different atoms. Among all entries of the 2 rows of one grid index, the atoms of each owner (atoms o * 16 to (o + 1) * 16 - 1) are named exactly 4 times or not at all.
All inputs are finite; a program needn't handle non-finite values.
Results may differ from a plain program's by a relative error of at most 0.0029.
Values may be sent and summed in bfloat16 or wider, within the bound.
No kernel may reach another device: no remote copies, remote signals or barrier semaphores. Data moves between devices by JAX's collectives and lax.ppermute only.
A program may use at most 128 MiB of HBM per device.

v0:
```python
import functools

import jax
import jax.numpy as jnp
from jax import lax
from jax.experimental import pallas as pl
from jax.experimental.pallas import tpu as pltpu
from jax.sharding import PartitionSpec as P

exchange_coef = -0.9847450218426965
lanes = 128
big_vmem = 60 * 1024 * 1024


def gather_matrix(rows, atoms, pad):
    count = atoms * pad
    lane = lax.broadcasted_iota(jnp.int32, (1, count), 1)
    place = jnp.full((1, count), -1, jnp.int32)
    start = 0
    for a in range(atoms):
        inner = lane - a * pad
        place = jnp.where((inner >= 0) & (inner < rows(a)), start + inner, place)
        start = start + rows(a)
    packed = lax.broadcasted_iota(jnp.int32, (count, count), 0)
    return jnp.where(packed == place, 1.0, 0.0).astype(jnp.bfloat16)


def spread_matrix(rows, atoms, pad):
    inner = lax.broadcasted_iota(jnp.int32, (pad, atoms * pad), 0)
    packed = lax.broadcasted_iota(jnp.int32, (pad, atoms * pad), 1)
    parts = []
    start = 0
    for a in range(atoms):
        parts.append(jnp.where((packed == start + inner) & (inner < rows(a)), 1.0, 0.0))
        start = start + rows(a)
    return jnp.concatenate(parts, axis=0).astype(jnp.bfloat16)


def pack_kernel(groups, per, rows_ref, coef_ref, main_ref, spill_ref):
    atoms, pad, band_dev = coef_ref.shape
    n, keep, width = main_ref.shape
    matrix = gather_matrix(lambda a: rows_ref[a], atoms, pad)
    for j in range(n):
        used = max(0, min(width, band_dev - j * width))
        if used:
            value = coef_ref[:, :, j * width : j * width + used].reshape(atoms * pad, used)
            packed = jnp.dot(matrix, value, preferred_element_type=jnp.float32)
            packed = packed.astype(jnp.bfloat16)
            main_ref[j, :, :used] = packed[:keep]
            spill_ref[j, :, :used] = packed[keep:]
        if used < width:
            main_ref[j, :, used:] = jnp.zeros((keep, width - used), jnp.bfloat16)
            spill_ref[j, :, used:] = jnp.zeros((atoms * pad - keep, width - used), jnp.bfloat16)


def unpack_kernel(groups, per, offsets, rows_ref, at_ref, spill_ref, *refs):
    in_refs, (out_ref, values, sems) = refs[: len(offsets)], refs[-3:]
    me = at_ref[0]
    atoms, pad, _ = out_ref.shape
    matrix = spread_matrix(lambda a: rows_ref[a], atoms, pad)
    whole, rest = groups // per, groups % per * lanes
    copies = []
    for index, in_ref in enumerate(in_refs):
        peer = me ^ offsets[index]
        packed = jnp.concatenate([in_ref[...], spill_ref[peer]], axis=0)
        value = jnp.dot(matrix, packed, preferred_element_type=jnp.float32)
        values[index] = value.reshape(values.shape[1:])
        start = pl.multiple_of(peer * (per * lanes), lanes)
        for used, there in ((per * lanes, peer < whole), (rest, peer == whole)):
            if used:
                target = out_ref.at[:, :, pl.ds(jnp.where(there, start, 0), used)]
                copy = pltpu.make_async_copy(
                    values.at[index, :, :, :used], target, sems.at[index]
                )
                copies.append((there, copy))
                pl.when(there)(copy.start)
    for there, copy in copies:
        pl.when(there)(copy.wait)


def prep_kernel(piece, at_ref, touch_ref, rows_ref, outer_ref, basis_ref, out_ref, meta, sem):
    beta = at_ref[1]
    tiles_dev, touch_len = touch_ref.shape
    atoms = rows_ref.shape[1]
    start = pl.multiple_of(beta * piece, piece)
    copy = pltpu.make_async_copy(basis_ref.at[pl.ds(start, piece)], out_ref.at[:piece], sem)
    copy.start()
    meta[...] = jnp.zeros_like(meta)
    rest = outer_ref[...]
    for part in range(3):
        rounded = rest.astype(jnp.bfloat16).astype(jnp.float32)
        meta[part * tiles_dev : (part + 1) * tiles_dev, :] = rounded
        rest = rest - rounded
    ids = touch_ref[...]
    row = 3 * tiles_dev
    meta[row : row + tiles_dev, :touch_len] = (ids & 255).astype(jnp.float32)
    row += tiles_dev
    meta[row : row + tiles_dev, :touch_len] = (ids >> 8).astype(jnp.float32)
    row += tiles_dev
    meta[row : row + 1, :atoms] = rows_ref[...].astype(jnp.float32)
    out_ref[piece:] = meta[...].astype(jnp.bfloat16)
    copy.wait()


def weights_kernel(groups, at_ref, weight_ref, after_ref, across_ref, down_ref):
    per = across_ref.shape[1] // lanes
    for q in range(per):
        k = at_ref[0] * per + q
        start = pl.multiple_of(jnp.minimum(k, groups - 1) * lanes, lanes)
        value = jnp.where(k < groups, weight_ref[:, pl.ds(start, lanes)], 0.0)
        across_ref[:, q * lanes : (q + 1) * lanes] = value
        down_ref[q * lanes : (q + 1) * lanes, :] = jnp.broadcast_to(value, (lanes, lanes)).T


def tables_kernel(piece, tiles_dev, touch_len, keep, *refs):
    in_refs, outs = refs[:-6], refs[-6:]
    outer_ref, touch_ref, rows_ref, more_ref, raw, sems = outs
    low = len(in_refs) // 2
    copies = []
    for d in range(raw.shape[0]):
        y, k = d % low, d // low
        source = in_refs[2 * y + (k > 0)].at[max(k - 1, 0), piece:]
        copies.append(pltpu.make_async_copy(source, raw.at[d], sems.at[d]))
    for copy in copies:
        copy.start()
    for copy in copies:
        copy.wait()
    most = jnp.zeros((1, 1), jnp.float32)
    for d in range(raw.shape[0]):
        value = raw[d].astype(jnp.float32)
        span = slice(d * tiles_dev, (d + 1) * tiles_dev)
        parts = [value[p * tiles_dev : (p + 1) * tiles_dev] for p in range(5)]
        outer_ref[span, :] = parts[0] + parts[1] + parts[2]
        touch_ref[span, :] = (parts[3] + 256.0 * parts[4])[:, :touch_len].astype(jnp.int32)
        counts = value[5 * tiles_dev : 5 * tiles_dev + 1, : rows_ref.shape[1]]
        rows_ref[d : d + 1, :] = counts.astype(jnp.int32)
        most = jnp.maximum(most, jnp.sum(counts, axis=1, keepdims=True))
    more_ref[...] = (most > keep).astype(jnp.int32)


def load_basis(basis_refs, basis, sems):
    m = basis.shape[1]
    copies = []
    for index, ref in enumerate(basis_refs):
        part, y, e = index % 2, index // 2 // m, index // 2 % m
        target = basis.at[y, e, part : part + ref.shape[0]]
        copies.append(pltpu.make_async_copy(ref, target, sems.at[index]))
    for copy in copies:
        copy.start()
    return copies


def tile_blocks(touch_ref, index, blocks):
    atoms, touch_len = blocks.shape[1], touch_ref.shape[1]
    ids = [touch_ref[index, s] for s in range(touch_len)]
    return jnp.concatenate([blocks[a // atoms, a % atoms] for a in ids], axis=0)


def tile_basis(beta, index, first, tiles_dev, piece, basis):
    width, m = basis.shape[:2]
    slot, column = index % tiles_dev, index // tiles_dev
    y, k = column % width, column // width
    count = m // tiles_dev
    parts = [basis[y, (slot * count + c) ^ beta, k, :piece] for c in range(count)]
    return jnp.concatenate(parts, axis=0), y, k, slot


def forward_kernel(plan, piece, scale, touch_ref, rows_ref, at_ref, weight_ref, *refs):
    n, k, low, tiles_dev, first = plan
    me, beta = at_ref[0], at_ref[1]
    if first:
        before_ref, block_ref, basis_refs = refs[0], refs[1], refs[2 : 2 + k]
        out_ref, blocks, basis, sems = refs[2 + k :]
    else:
        received, basis_refs = refs[:-4][: -k], refs[:-4][-k:]
        out_ref, blocks, basis, sems = refs[-4:]
    _, atoms, pad, width = blocks.shape
    copies = load_basis(basis_refs, basis, sems)
    if first:
        copies.append(pltpu.make_async_copy(block_ref, blocks, sems.at[k]))
        copies[-1].start()
        out_ref[...] = before_ref[...]
    else:
        for d in range(n):
            owner = me ^ d
            matrix = spread_matrix(lambda a: rows_ref[d, a], atoms, pad)
            packed = jnp.concatenate([ref[owner] for ref in received], axis=0)
            matrix = matrix[:, : packed.shape[0]]
            value = jnp.dot(matrix, packed, preferred_element_type=jnp.float32)
            blocks[owner] = value.astype(jnp.bfloat16).reshape(atoms, pad, width)
        out_ref[...] = jnp.zeros_like(out_ref)
    for copy in copies:
        copy.wait()

    def step(index, carry):
        values, y, z, slot = tile_basis(beta, index, first, tiles_dev, piece, basis)
        d = z * low + first + y
        part = tile_blocks(touch_ref, d * tiles_dev + slot, blocks)
        product = lax.dot_general(
            part, values, (((0,), (0,)), ((), ())), preferred_element_type=jnp.float32
        )
        orbital = product.astype(jnp.bfloat16).astype(jnp.float32)
        weight = jnp.concatenate([weight_ref[...]] * (orbital.shape[1] // lanes), axis=1)
        out_ref[pl.ds((d ^ me) * tiles_dev + slot, 1), :] = scale * jnp.sum(
            weight * orbital * orbital, axis=0, keepdims=True
        )
        return carry

    lax.fori_loop(0, basis.shape[0] * basis.shape[2] * tiles_dev, step, 0, unroll=4)


def backward_kernel(
    n, k, tiles_dev, piece, touch_ref, rows_ref, at_ref, weight_ref, outer_ref, local_ref, *refs
):
    basis_refs, block_ref = refs[:k], refs[k]
    out_refs = refs[k + 1 : k + 1 + n]
    spill_ref, blocks, basis, total, sems = refs[k + 1 + n :]
    me, beta = at_ref[0], at_ref[1]
    tile_count, touch_len = touch_ref.shape
    _, atoms, pad, width = blocks.shape
    copies = load_basis(basis_refs, basis, sems)
    copies.append(pltpu.make_async_copy(block_ref, blocks, sems.at[k]))
    copies[-1].start()
    total[...] = jnp.zeros_like(total)
    weight = weight_ref[...]
    for copy in copies:
        copy.wait()

    def step(index, carry):
        values, y, z, slot = tile_basis(beta, index, 0, tiles_dev, piece, basis)
        d = z * basis.shape[0] + y
        row = d * tiles_dev + slot
        part = tile_blocks(touch_ref, row, blocks)
        potential = (
            outer_ref[pl.ds(row, 1), :] + local_ref[pl.ds((d ^ me) * tiles_dev + slot, 1), :]
        )
        scaled = (values.astype(jnp.float32) * potential).astype(jnp.bfloat16)
        couple = lax.dot_general(
            scaled, values, (((1,), (1,)), ((), ())), preferred_element_type=jnp.float32
        )
        high = couple.astype(jnp.bfloat16)
        low = (couple - high.astype(jnp.float32)).astype(jnp.bfloat16)
        product = jnp.dot(high, part, preferred_element_type=jnp.float32) + jnp.dot(
            low, part, preferred_element_type=jnp.float32
        )
        for s in range(touch_len):
            total[touch_ref[row, s]] += product[s * pad : (s + 1) * pad]
        return carry

    lax.fori_loop(0, tile_count, step, 0, unroll=4)
    for d, out_ref in enumerate(out_refs):
        owner = me ^ d
        matrix = gather_matrix(lambda a: rows_ref[d, a], atoms, pad)
        value = total[pl.ds(owner * atoms, atoms)].reshape(atoms * pad, width)
        value = (weight * value).astype(jnp.bfloat16)
        packed = jnp.dot(matrix, value, preferred_element_type=jnp.float32).astype(jnp.bfloat16)
        out_ref[...] = packed[: out_ref.shape[0]]
        spill_ref[owner] = packed[out_ref.shape[0] :]


smem = pl.BlockSpec(memory_space=pltpu.SMEM)
vmem = pl.BlockSpec(memory_space=pltpu.VMEM)
anywhere = pl.BlockSpec(memory_space=pl.ANY)


def swap(value, axis, offset):
    size = lax.axis_size(axis)
    return lax.ppermute(value, axis, [(i, i ^ offset) for i in range(size)])


def exchange(parts):
    return [parts[0]] + [swap(parts[d], "grid", d) for d in range(1, len(parts))]


def all_sum(value):
    for axis in ("band", "grid"):
        offset = 1
        while offset < lax.axis_size(axis):
            value = value + swap(value, axis, offset)
            offset *= 2
    return value


def body(coefficients, block_rows, touch_atoms, basis_values, outer_field, occupations):
    n = lax.axis_size("grid")
    m = lax.axis_size("band")
    me = lax.axis_index("grid").astype(jnp.int32)
    beta = lax.axis_index("band").astype(jnp.int32)
    atoms, pad, band_dev = coefficients.shape
    tiles_dev, touch_len = touch_atoms.shape
    points = basis_values.shape[2]
    slots = basis_values.shape[1]
    tile_count = tiles_dev * n
    groups = band_dev // lanes
    per = (groups + n - 1) // n
    width = per * lanes
    params = pltpu.CompilerParams(vmem_limit_bytes=big_vmem)
    at = jnp.stack([me, beta])

    keep = atoms * pad * 13 // 16

    def across(value):
        return lax.all_to_all(value, "grid", split_axis=0, concat_axis=0, tiled=True)

    piece = tiles_dev * slots // m
    extra = -(-(5 * tiles_dev + 1) // 16) * 16
    low = 1 << ((n.bit_length() - 1) // 2)
    message = pl.pallas_call(
        functools.partial(prep_kernel, piece),
        out_shape=jax.ShapeDtypeStruct((piece + extra, points), jnp.bfloat16),
        in_specs=[smem, vmem, vmem, vmem, anywhere],
        out_specs=vmem,
        scratch_shapes=[pltpu.VMEM((extra, points), jnp.float32), pltpu.SemaphoreType.DMA],
        compiler_params=params,
        name="prep",
    )(
        at,
        touch_atoms,
        block_rows.reshape(1, atoms),
        outer_field,
        basis_values.reshape(tiles_dev * slots, points),
    )
    size = n // low
    pieces = {}

    def widen(h):
        for y in range(1, low):
            pieces[y, 0, h] = swap(pieces[0, 0, h], "grid", y)

    column = [message] + [swap(message, "grid", low * k) for k in range(1, size)]
    pieces[0, 0, 0] = message[None]
    widen(0)
    sent, spill = pl.pallas_call(
        functools.partial(pack_kernel, groups, per),
        out_shape=[
            jax.ShapeDtypeStruct((n, keep, width), jnp.bfloat16),
            jax.ShapeDtypeStruct((n, atoms * pad - keep, width), jnp.bfloat16),
        ],
        in_specs=[smem, vmem],
        out_specs=[vmem, vmem],
        compiler_params=params,
        name="pack",
    )(block_rows, coefficients)
    sent, spill, column, pieces = lax.optimization_barrier((sent, spill, column, pieces))
    got = across(sent)
    parts = [0, 1]
    pieces[0, 0, 1] = jnp.stack(column[1:])
    widen(1)
    cover = pl.CostEstimate(flops=0, bytes_accessed=1 << 27, transcendentals=0)
    weight, weight_down = pl.pallas_call(
        functools.partial(weights_kernel, groups),
        out_shape=[
            jax.ShapeDtypeStruct((1, width), jnp.float32),
            jax.ShapeDtypeStruct((width, lanes), jnp.float32),
        ],
        in_specs=[smem, vmem, anywhere],
        out_specs=[vmem] * 2,
        compiler_params=params,
        cost_estimate=cover,
        name="weights",
    )(at, occupations[None, :], pieces[0, 0, 1])
    last = [(y, x, 1) for y in range(1, low) for x in range(2, m, 2)]
    for h in parts:
        for y in range(low):
            for x in range(2, m, 2):
                if (y, x, h) not in last:
                    pieces[y, x, h] = swap(pieces[y, 0, h], "band", x)
    pieces, weight, weight_down = lax.optimization_barrier((pieces, weight, weight_down))
    for y, x, h in last:
        pieces[y, x, h] = swap(pieces[y, 0, h], "band", x)
    tables = [pieces[y, 0, h] for y in range(low) for h in parts]
    outer, touch, rows, more = pl.pallas_call(
        functools.partial(tables_kernel, piece, tiles_dev, touch_len, keep),
        out_shape=[
            jax.ShapeDtypeStruct((tile_count, points), jnp.float32),
            jax.ShapeDtypeStruct((tile_count, touch_len), jnp.int32),
            jax.ShapeDtypeStruct((n, atoms), jnp.int32),
            jax.ShapeDtypeStruct((1, 1), jnp.int32),
        ],
        in_specs=[anywhere] * len(tables),
        out_specs=[vmem] * 4,
        scratch_shapes=[
            pltpu.VMEM((n, extra, points), jnp.bfloat16),
            pltpu.SemaphoreType.DMA((n,)),
        ],
        compiler_params=params,
        name="tables",
    )(*tables)
    more = more[0, 0] > 0

    def rest(value):
        return lax.cond(more, across, lambda same: same, value)

    for y, x, h in list(pieces):
        if (y, x, h) not in last:
            pieces[y, x + 1, h] = swap(pieces[y, x, h], "band", 1)
    all_bands = band_dev * m
    held = jax.ShapeDtypeStruct((n, atoms, pad, width), jnp.bfloat16)
    value = jax.ShapeDtypeStruct((tile_count, points), jnp.float32)
    near, far = range(1), range(1, low)

    def basis_of(columns):
        return [pieces[y, e, h] for y in columns for e in range(m) for h in parts]

    def forward(columns, inputs):
        arrays = basis_of(columns)
        first = columns[0]
        plan = (n, len(arrays), low, tiles_dev, first)
        room = [
            pltpu.VMEM((len(columns), m, size, piece + extra, points), jnp.bfloat16),
            pltpu.SemaphoreType.DMA((1 + len(arrays),)),
        ]
        places = [vmem, anywhere] if first else [vmem] * len(inputs)
        return pl.pallas_call(
            functools.partial(forward_kernel, plan, piece, 1.0 / all_bands),
            out_shape=value if first else [value, held],
            in_specs=[smem, smem, smem, vmem] + places + [anywhere] * len(arrays),
            out_specs=vmem if first else [vmem, vmem],
            scratch_shapes=[pltpu.VMEM(held.shape, held.dtype)] * (first > 0) + room,
            compiler_params=params,
            cost_estimate=pl.CostEstimate(
                flops=2 * tile_count // low * len(columns) * slots * width * points,
                bytes_accessed=1 << 27,
                transcendentals=0,
            ),
            name="forward",
        )(touch, rows, at, weight_down, *inputs, *arrays)

    partial_value, blocks = forward(near, [got])
    ends, partial_value, blocks = lax.optimization_barrier(
        ([pieces[k] for k in last], partial_value, blocks)
    )
    for (y, x, h), end in zip(last, ends):
        pieces[y, x, h] = end
        pieces[y, x + 1, h] = swap(end, "band", 1)
    partial_value = forward(far, [partial_value, blocks])

    def again(spill, *_):
        once, blocks = forward(near, [got, across(spill)])
        return forward(far, [once, blocks]), blocks

    partial_value, blocks = lax.cond(
        more, again, lambda spill, *same: same, spill, partial_value, blocks
    )
    basis = basis_of(range(low))
    count = len(basis)
    scratch = [
        pltpu.VMEM((n, atoms, pad, width), jnp.bfloat16),
        pltpu.VMEM((low, m, n // low, piece + extra, points), jnp.bfloat16),
    ]
    sems = pltpu.SemaphoreType.DMA((1 + count,))
    density = all_sum(partial_value)
    local = exchange_coef * jnp.cbrt(density)
    *back, spill = pl.pallas_call(
        functools.partial(backward_kernel, n, count, tiles_dev, piece),
        out_shape=[jax.ShapeDtypeStruct((keep, width), jnp.bfloat16)] * n
        + [jax.ShapeDtypeStruct((n, atoms * pad - keep, width), jnp.bfloat16)],
        in_specs=[smem, smem, smem, vmem, vmem, vmem] + [anywhere] * (1 + count),
        out_specs=[vmem] * (n + 1),
        scratch_shapes=scratch + [pltpu.VMEM((n * atoms, pad, width), jnp.float32), sems],
        compiler_params=params,
        name="backward",
    )(touch, rows, at, weight, outer, local, *basis, blocks)
    returned = exchange(back)
    spill = rest(spill)
    gradient = None
    for offsets in (range(n // 2), range(n // 2, n)):
        before = [] if gradient is None else [gradient]
        gradient = pl.pallas_call(
            functools.partial(unpack_kernel, groups, per, tuple(offsets)),
            out_shape=jax.ShapeDtypeStruct((atoms, pad, band_dev), jnp.float32),
            in_specs=[smem, smem] + [vmem] * (1 + len(offsets)) + [anywhere] * len(before),
            out_specs=anywhere,
            scratch_shapes=[
                pltpu.VMEM((len(offsets), atoms, pad, width), jnp.float32),
                pltpu.SemaphoreType.DMA((len(offsets),)),
            ],
            input_output_aliases={3 + len(offsets): 0} if before else {},
            compiler_params=params,
            cost_estimate=pl.CostEstimate(flops=0, bytes_accessed=1 << 22, transcendentals=0),
            name="unpack",
        )(block_rows, at, spill, *[returned[d] for d in offsets], *before)
    own_density = lax.dynamic_slice_in_dim(density, me * tiles_dev, tiles_dev, 0)
    return (gradient, own_density)


def solution(mesh):
    placed = (
        P("grid", None, "band"),
        P("grid"),
        P("grid", None),
        P("grid", None, None),
        P("grid", None),
        P("band"),
    )
    return jax.shard_map(
        body,
        mesh=mesh,
        in_specs=placed,
        out_specs=(P("grid", None, "band"), P("grid", None)),
        check_vma=False,
    )
```

profile of v0, /device:TPU:8, one launch (start us, length us, event | category | flops | bytes accessed | tf_op | source)
XLA Modules:
  0.0 156.6 jit_solution(15349869134587835064)
XLA Ops:
  8.0 3.5 %pack.1 = (bf16[8,208,512]{2,1,0:T(8,128)(2,1)}, bf16[8,48,512]{2,1,0:T(8,128)(2,1)}) custom-call(s32[16]{0:T(128)} %rows_ref.5, bf16[16,16,3840]{2,1,0:T(8,128)(2,1)} %coef_ref.1), custom_call_target="tpu_custom_call" | custom-call | tf_op jit(solution)/shard_map/pack/pallas_call | solution.py:333
  11.6 7.4 %collective-permute-done.2 = bf16[144,640]{1,0:T(8,128)(2,1)S(1)} collective-permute-done((bf16[144,640]{1,0:T(8,128)(2,1)S(1)}, bf16[144,640]{1,0:T(8,128)(2,1)S(1)}, u32[]{:S(2)}, u32[]{:S(2)}) %collective-permute-start.2) | collective-permute-done | bytes 184352 | tf_op jit(solution)/shard_map/ppermute | solution.py:268
  19.0 2.0 %collective-permute-done.1 = bf16[144,640]{1,0:T(8,128)(2,1)S(1)} collective-permute-done((bf16[144,640]{1,0:T(8,128)(2,1)S(1)}, bf16[144,640]{1,0:T(8,128)(2,1)S(1)}, u32[]{:S(2)}, u32[]{:S(2)}) %collective-permute-start.1) | collective-permute-done | bytes 184352 | tf_op jit(solution)/shard_map/ppermute | solution.py:268
  21.0 6.1 %all-to-all-start.2 = ((bf16[8,208,512]{2,1,0:T(8,128)(2,1)}), bf16[8,208,512]{2,1,0:T(8,128)(2,1)S(1)}, u32[]{:S(2)}, u32[]{:S(2)}) async-start(bf16[8,208,512]{2,1,0:T(8,128)(2,1)} %get-tuple-element.138), calls=%async_computation.2 | async-start | bytes 3407872 | tf_op jit(solution)/shard_map/all_to_all | solution.py:303
  35.2 12.2 %collective-permute-done.4.refs_5_.refs_4_ = bf16[1,144,640]{2,1,0:T(8,128)(2,1)S(1)} collective-permute-done((bf16[1,144,640]{2,1,0:T(8,128)(2,1)S(1)}, bf16[1,144,640]{2,1,0:T(8,128)(2,1)S(1)}, u32[]{:S(2)}, u32[]{:S(2)}) %collective-permute-start.4) | collective-permute-done | bytes 184352 | tf_op jit(solution)/shard_map/ppermute | solution.py:268
  49.4 7.0 %collective-permute-done.6.refs_3_.refs_9_ = bf16[3,144,640]{2,1,0:T(8,128)(2,1)S(1)} collective-permute-done((bf16[3,144,640]{2,1,0:T(8,128)(2,1)S(1)}, bf16[3,144,640]{2,1,0:T(8,128)(2,1)S(1)}, u32[]{:S(2)}, u32[]{:S(2)}) %collective-permute-start.6) | collective-permute-done | bytes 552992 | tf_op jit(solution)/shard_map/ppermute | solution.py:268
  60.6 2.3 %all-to-all-done.2.refs_0_ = bf16[8,208,512]{2,1,0:T(8,128)(2,1)S(1)} async-done(((bf16[8,208,512]{2,1,0:T(8,128)(2,1)}), bf16[8,208,512]{2,1,0:T(8,128)(2,1)S(1)}, u32[]{:S(2)}, u32[]{:S(2)}) %all-to-all-start.2) | async-done | bytes 1703968 | tf_op jit(solution)/shard_map/all_to_all | solution.py:303
  62.9 6.9 %forward.6 = (f32[16,640]{1,0:T(8,128)}, bf16[8,16,16,512]{3,2,1,0:T(8,128)(2,1)}) custom-call(s32[16,16]{1,0:T(8,128)S(1)} %get-tuple-element.133.touch_ref, s32[8,16]{1,0:T(8,128)} %get-tuple-element.134.rows_ref, s32[2]{0:T(128)} %copy-done.15, f32[512,128]{1,0:T(8,128)} %get-tuple-element.137.weight_ref, ...), custom_call_target="tpu_custom_call" | custom-call | flops 1342177280 | bytes 134217728 | tf_op jit(solution)/shard_map/forward/pallas_call | solution.py:414
  74.6 6.8 %forward.7 = f32[16,640]{1,0:T(8,128)} custom-call(s32[16,16]{1,0:T(8,128)S(1)} %get-tuple-element.133.touch_ref, s32[8,16]{1,0:T(8,128)S(1)} %copy-done.14, s32[2]{0:T(128)S(1)} %copy-done.16, f32[512,128]{1,0:T(8,128)} %get-tuple-element.137.weight_ref, f32[16,640]{1,0:T(8,128)} %get-tuple-element.143.refs_0_, ...), custom_call_target="tpu_custom_call" | custom-call | flops 1342177280 | bytes 134217728 | tf_op jit(solution)/shard_map/forward/pallas_call | solution.py:414
  85.4 2.5 %collective-permute-done.18 = f32[16,640]{1,0:T(8,128)S(1)} collective-permute-done((f32[16,640]{1,0:T(8,128)S(1)}, f32[16,640]{1,0:T(8,128)S(1)}, u32[]{:S(2)}, u32[]{:S(2)}) %collective-permute-start.18) | collective-permute-done | bytes 40992 | tf_op jit(solution)/shard_map/ppermute | solution.py:268
  87.9 2.5 %collective-permute-start.19 = (f32[16,640]{1,0:T(8,128)S(1)}, f32[16,640]{1,0:T(8,128)S(1)}, u32[]{:S(2)}, u32[]{:S(2)}) collective-permute-start(f32[16,640]{1,0:T(8,128)S(1)} %add.19), channel_id=1, source_target_pairs={{0,1},{1,0},{2,3},{3,2},{4,5},{5,4},{6,7},{7,6},{8,9},{9,8},{10,11... | collective-permute-start | bytes 122888 | tf_op jit(solution)/shard_map/ppermute | solution.py:268
  92.4 2.0 %collective-permute-start.20 = (f32[16,640]{1,0:T(8,128)S(1)}, f32[16,640]{1,0:T(8,128)S(1)}, u32[]{:S(2)}, u32[]{:S(2)}) collective-permute-start(f32[16,640]{1,0:T(8,128)S(1)} %add.20), channel_id=1, source_target_pairs={{0,2},{1,3},{2,0},{3,1},{4,6},{5,7},{6,4},{7,5},{8,10},{9,11},{10,... | collective-permute-start | bytes 122888 | tf_op jit(solution)/shard_map/ppermute | solution.py:268
  96.4 3.9 %collective-permute-start.21 = (f32[16,640]{1,0:T(8,128)S(1)}, f32[16,640]{1,0:T(8,128)S(1)}, u32[]{:S(2)}, u32[]{:S(2)}) collective-permute-start(f32[16,640]{1,0:T(8,128)S(1)} %add.21), channel_id=1, source_target_pairs={{0,4},{1,5},{2,6},{3,7},{4,0},{5,1},{6,2},{7,3},{8,12},{9,13},{10,... | collective-permute-start | bytes 122888 | tf_op jit(solution)/shard_map/ppermute | solution.py:268
  100.2 2.0 %collective-permute-done.21 = f32[16,640]{1,0:T(8,128)S(1)} collective-permute-done((f32[16,640]{1,0:T(8,128)S(1)}, f32[16,640]{1,0:T(8,128)S(1)}, u32[]{:S(2)}, u32[]{:S(2)}) %collective-permute-start.21) | collective-permute-done | bytes 40992 | tf_op jit(solution)/shard_map/ppermute | solution.py:268
  102.9 12.1 %backward.1 = (bf16[208,512]{1,0:T(8,128)(2,1)}, bf16[208,512]{1,0:T(8,128)(2,1)}, bf16[208,512]{1,0:T(8,128)(2,1)}, bf16[208,512]{1,0:T(8,128)(2,1)}, bf16[208,...) custom-call(s32[16,16]{1,0:T(8,128)S(1)} %get-tuple-element.133.touc, ...), custom_call_target="tpu_custom_call" | custom-call | tf_op jit(solution)/shard_map/backward/pallas_call | solution.py:454
  117.1 2.2 %collective-permute-start.22 = (bf16[208,512]{1,0:T(8,128)(2,1)}, bf16[208,512]{1,0:T(8,128)(2,1)S(1)}, u32[]{:S(2)}, u32[]{:S(2)}) collective-permute-start(bf16[208,512]{1,0:T(8,128)(2,1)} %get-tuple-element.151), channel_id=1, source_target_pairs={{0,4},{1,5},{2,6},{3,7},{4,0},{5,1},{6,2},{7,3},{8,12},{9,13},{10,... | collective-permute-start | bytes 638984 | tf_op jit(solution)/shard_map/ppermute | solution.py:268
  122.5 2.3 %collective-permute-start.24 = (bf16[208,512]{1,0:T(8,128)(2,1)}, bf16[208,512]{1,0:T(8,128)(2,1)S(1)}, u32[]{:S(2)}, u32[]{:S(2)}) collective-permute-start(bf16[208,512]{1,0:T(8,128)(2,1)} %get-tuple-element.153), channel_id=1, source_target_pairs={{0,6},{1,7},{2,4},{3,5},{4,2},{5,3},{6,0},{7,1},{8,14},{9,15},{10,... | collective-permute-start | bytes 638984 | tf_op jit(solution)/shard_map/ppermute | solution.py:268
  125.7 2.3 %collective-permute-start.25 = (bf16[208,512]{1,0:T(8,128)(2,1)}, bf16[208,512]{1,0:T(8,128)(2,1)S(1)}, u32[]{:S(2)}, u32[]{:S(2)}) collective-permute-start(bf16[208,512]{1,0:T(8,128)(2,1)} %get-tuple-element.154), channel_id=1, source_target_pairs={{0,7},{1,6},{2,5},{3,4},{4,3},{5,2},{6,1},{7,0},{8,15},{9,14},{10,... | collective-permute-start | bytes 638984 | tf_op jit(solution)/shard_map/ppermute | solution.py:268
  128.5 9.6 %collective-permute-done.28.refs_3_ = bf16[208,512]{1,0:T(8,128)(2,1)S(1)} collective-permute-done((bf16[208,512]{1,0:T(8,128)(2,1)}, bf16[208,512]{1,0:T(8,128)(2,1)S(1)}, u32[]{:S(2)}, u32[]{:S(2)}) %collective-permute-start.28) | collective-permute-done | bytes 213024 | tf_op jit(solution)/shard_map/ppermute | solution.py:268
  138.9 2.8 %unpack.2.refs_4_ = f32[16,16,3840]{2,1,0:T(8,128)} custom-call(s32[16]{0:T(128)} %rows_ref.5, s32[2]{0:T(128)S(1)} %copy-done.17, bf16[8,48,512]{2,1,0:T(8,128)(2,1)S(1)} %get-tuple-element.166.spill_ref, bf16[208,512]{1,0:T(8,128)(2,1)} %get-tuple-element.155.refs_0_, bf16[208,512]{1,0:T(8,128)(2,1)} %copy-done.9, bf16[208,512]{1,0:T(8,128)(2,1)} %copy-done.11, ...), custom_call_target="tpu_custom_call" | custom-call | bytes 4194304 | tf_op jit(solution)/shard_map/unpack/pallas_call | solution.py:469
  141.7 2.7 %collective-permute-done.23.refs_1_ = bf16[208,512]{1,0:T(8,128)(2,1)S(1)} collective-permute-done((bf16[208,512]{1,0:T(8,128)(2,1)}, bf16[208,512]{1,0:T(8,128)(2,1)S(1)}, u32[]{:S(2)}, u32[]{:S(2)}) %collective-permute-start.23) | collective-permute-done | bytes 213024 | tf_op jit(solution)/shard_map/ppermute | solution.py:268
  144.4 5.4 %collective-permute-done.24.refs_2_ = bf16[208,512]{1,0:T(8,128)(2,1)S(1)} collective-permute-done((bf16[208,512]{1,0:T(8,128)(2,1)}, bf16[208,512]{1,0:T(8,128)(2,1)S(1)}, u32[]{:S(2)}, u32[]{:S(2)}) %collective-permute-start.24) | collective-permute-done | bytes 213024 | tf_op jit(solution)/shard_map/ppermute | solution.py:268
  149.8 3.2 %collective-permute-done.25.refs_3_ = bf16[208,512]{1,0:T(8,128)(2,1)S(1)} collective-permute-done((bf16[208,512]{1,0:T(8,128)(2,1)}, bf16[208,512]{1,0:T(8,128)(2,1)S(1)}, u32[]{:S(2)}, u32[]{:S(2)}) %collective-permute-start.25) | collective-permute-done | bytes 213024 | tf_op jit(solution)/shard_map/ppermute | solution.py:268
  153.7 2.8 %unpack.3 = f32[16,16,3840]{2,1,0:T(8,128)} custom-call(s32[16]{0:T(128)} %rows_ref.5, s32[2]{0:T(128)S(1)} %copy-done.17, bf16[8,48,512]{2,1,0:T(8,128)(2,1)S(1)} %get-tuple-element.166.spill_ref, bf16[208,512]{1,0:T(8,128)(2,1)} %copy-done.7, bf16[208,512]{1,0:T(8,128)(2,1)} %copy-done.8, ...), custom_call_target="tpu_custom_call", output_to_operand_aliasing={{}: (7, {})} | custom-call | bytes 4194304 | tf_op jit(solution)/shard_map/unpack/pallas_call | solution.py:469
  (92 shorter events, 42.3 us)
Async XLA Ops:
  2.4 9.2 %collective-permute-start.3 = (bf16[1,144,640]{2,1,0:T(8,128)(2,1)S(1)}, bf16[1,144,640]{2,1,0:T(8,128)(2,1)S(1)}, u32[]{:S(2)}, u32[]{:S(2)}) collective-permute-start(bf16[1,144,640]{2,1,0:T(8,128)(2,1)S(1)} %bitcast.9), channel_id=1, source_target_pairs={{0,1},{1,0},{2,3},{3,2},{4,5},{5,4},{6,7},{7,6},{8,9},{9,8},{10,11... | collective-permute-start | bytes 552968 | tf_op jit(solution)/shard_map/ppermute | solution.py:268
  4.0 15.0 %collective-permute-start.2 = (bf16[144,640]{1,0:T(8,128)(2,1)S(1)}, bf16[144,640]{1,0:T(8,128)(2,1)S(1)}, u32[]{:S(2)}, u32[]{:S(2)}) collective-permute-start(bf16[144,640]{1,0:T(8,128)(2,1)S(1)} %prep.1), channel_id=1, source_target_pairs={{0,6},{1,7},{2,4},{3,5},{4,2},{5,3},{6,0},{7,1},{8,14},{9,15},{10,... | collective-permute-start | bytes 552968 | tf_op jit(solution)/shard_map/ppermute | solution.py:268
  5.6 15.5 %collective-permute-start.1 = (bf16[144,640]{1,0:T(8,128)(2,1)S(1)}, bf16[144,640]{1,0:T(8,128)(2,1)S(1)}, u32[]{:S(2)}, u32[]{:S(2)}) collective-permute-start(bf16[144,640]{1,0:T(8,128)(2,1)S(1)} %prep.1), channel_id=1, source_target_pairs={{0,4},{1,5},{2,6},{3,7},{4,0},{5,1},{6,2},{7,3},{8,12},{9,13},{10,... | collective-permute-start | bytes 552968 | tf_op jit(solution)/shard_map/ppermute | solution.py:268
  6.8 14.2 %collective-permute-start = (bf16[144,640]{1,0:T(8,128)(2,1)S(1)}, bf16[144,640]{1,0:T(8,128)(2,1)S(1)}, u32[]{:S(2)}, u32[]{:S(2)}) collective-permute-start(bf16[144,640]{1,0:T(8,128)(2,1)S(1)} %prep.1), channel_id=1, source_target_pairs={{0,2},{1,3},{2,0},{3,1},{4,6},{5,7},{6,4},{7,5},{8,10},{9,11},{10,... | collective-permute-start | bytes 552968 | tf_op jit(solution)/shard_map/ppermute | solution.py:268
  21.0 41.8 %all-to-all-start.2 = ((bf16[8,208,512]{2,1,0:T(8,128)(2,1)}), bf16[8,208,512]{2,1,0:T(8,128)(2,1)S(1)}, u32[]{:S(2)}, u32[]{:S(2)}) async-start(bf16[8,208,512]{2,1,0:T(8,128)(2,1)} %get-tuple-element.138), calls=%async_computation.2 | async-start | bytes 3407872 | tf_op jit(solution)/shard_map/all_to_all | solution.py:303
  27.2 29.2 %collective-permute-start.6 = (bf16[3,144,640]{2,1,0:T(8,128)(2,1)S(1)}, bf16[3,144,640]{2,1,0:T(8,128)(2,1)S(1)}, u32[]{:S(2)}, u32[]{:S(2)}) collective-permute-start(bf16[3,144,640]{2,1,0:T(8,128)(2,1)S(1)} %pad_maximum_fusion.after_ref.refs_1_.refs_2_), channel_id=1, source_target_pairs={{0,1},{1,0},{2,3},{3,2},{4,5},{5,4},{6,7},{7,6},{8,9},{9,8},{10,11... | collective-permute-start | bytes 1658888 | tf_op jit(solution)/shard_map/ppermute | solution.py:268
  28.7 27.7 %collective-permute-start.5 = (bf16[3,144,640]{2,1,0:T(8,128)(2,1)S(1)}, bf16[3,144,640]{2,1,0:T(8,128)(2,1)S(1)}, u32[]{:S(2)}, u32[]{:S(2)}) collective-permute-start(bf16[3,144,640]{2,1,0:T(8,128)(2,1)S(1)} %pad_maximum_fusion.after_ref.refs_1_.refs_2_), channel_id=1, source_target_pairs={{0,16},{8,24},{16,0},{24,8},{1,17},{9,25},{17,1},{25,9},{2,18},{10... | collective-permute-start | bytes 1658888 | tf_op jit(solution)/shard_map/ppermute | solution.py:268
  30.2 17.2 %collective-permute-start.4 = (bf16[1,144,640]{2,1,0:T(8,128)(2,1)S(1)}, bf16[1,144,640]{2,1,0:T(8,128)(2,1)S(1)}, u32[]{:S(2)}, u32[]{:S(2)}) collective-permute-start(bf16[1,144,640]{2,1,0:T(8,128)(2,1)S(1)} %bitcast.10), channel_id=1, source_target_pairs={{0,16},{8,24},{16,0},{24,8},{1,17},{9,25},{17,1},{25,9},{2,18},{10... | collective-permute-start | bytes 552968 | tf_op jit(solution)/shard_map/ppermute | solution.py:268
  30.8 18.6 %collective-permute-start.7 = (bf16[1,144,640]{2,1,0:T(8,128)(2,1)S(1)}, bf16[1,144,640]{2,1,0:T(8,128)(2,1)S(1)}, u32[]{:S(2)}, u32[]{:S(2)}) collective-permute-start(bf16[1,144,640]{2,1,0:T(8,128)(2,1)S(1)} %collective-permute-done.3.refs_2_.refs_8_), channel_id=1, source_target_pairs={{0,16},{8,24},{16,0},{24,8},{1,17},{9,25},{17,1},{25,9},{2,18},{10... | collective-permute-start | bytes 552968 | tf_op jit(solution)/shard_map/ppermute | solution.py:268
  56.4 4.1 %collective-permute-start.12 = (bf16[3,144,640]{2,1,0:T(8,128)(2,1)S(1)}, bf16[3,144,640]{2,1,0:T(8,128)(2,1)}, u32[]{:S(2)}, u32[]{:S(2)}) collective-permute-start(bf16[3,144,640]{2,1,0:T(8,128)(2,1)S(1)} %collective-permute-done.5.refs_6_.refs_5_), channel_id=1, source_target_pairs={{0,8},{8,0},{16,24},{24,16},{1,9},{9,1},{17,25},{25,17},{2,10},{10... | collective-permute-start | bytes 1658888 | tf_op jit(solution)/shard_map/ppermute | solution.py:268
  56.5 4.1 %collective-permute-start.10 = (bf16[3,144,640]{2,1,0:T(8,128)(2,1)S(1)}, bf16[3,144,640]{2,1,0:T(8,128)(2,1)}, u32[]{:S(2)}, u32[]{:S(2)}) collective-permute-start(bf16[3,144,640]{2,1,0:T(8,128)(2,1)S(1)} %pad_maximum_fusion.after_ref.refs_1_.refs_2_), channel_id=1, source_target_pairs={{0,8},{8,0},{16,24},{24,16},{1,9},{9,1},{17,25},{25,17},{2,10},{10... | collective-permute-start | bytes 1658888 | tf_op jit(solution)/shard_map/ppermute | solution.py:268
  57.0 14.5 %collective-permute-start.8 = (bf16[3,144,640]{2,1,0:T(8,128)(2,1)S(1)}, bf16[3,144,640]{2,1,0:T(8,128)(2,1)S(1)}, u32[]{:S(2)}, u32[]{:S(2)}) collective-permute-start(bf16[3,144,640]{2,1,0:T(8,128)(2,1)S(1)} %collective-permute-done.6.refs_3_.refs_9_), channel_id=1, source_target_pairs={{0,16},{8,24},{16,0},{24,8},{1,17},{9,25},{17,1},{25,9},{2,18},{10... | collective-permute-start | bytes 1658888 | tf_op jit(solution)/shard_map/ppermute | solution.py:268
  60.4 13.5 %collective-permute-start.14 = (bf16[3,144,640]{2,1,0:T(8,128)(2,1)S(1)}, bf16[3,144,640]{2,1,0:T(8,128)(2,1)}, u32[]{:S(2)}, u32[]{:S(2)}) collective-permute-start(bf16[3,144,640]{2,1,0:T(8,128)(2,1)S(1)} %collective-permute-done.6.refs_3_.refs_9_), channel_id=1, source_target_pairs={{0,8},{8,0},{16,24},{24,16},{1,9},{9,1},{17,25},{25,17},{2,10},{10... | collective-permute-start | bytes 1658888 | tf_op jit(solution)/shard_map/ppermute | solution.py:268
  83.9 4.0 %collective-permute-start.18 = (f32[16,640]{1,0:T(8,128)S(1)}, f32[16,640]{1,0:T(8,128)S(1)}, u32[]{:S(2)}, u32[]{:S(2)}) collective-permute-start(f32[16,640]{1,0:T(8,128)S(1)} %add.18), channel_id=1, source_target_pairs={{0,16},{8,24},{16,0},{24,8},{1,17},{9,25},{17,1},{25,9},{2,18},{10... | collective-permute-start | bytes 122888 | tf_op jit(solution)/shard_map/ppermute | solution.py:268
  87.9 4.5 %collective-permute-start.19 = (f32[16,640]{1,0:T(8,128)S(1)}, f32[16,640]{1,0:T(8,128)S(1)}, u32[]{:S(2)}, u32[]{:S(2)}) collective-permute-start(f32[16,640]{1,0:T(8,128)S(1)} %add.19), channel_id=1, source_target_pairs={{0,1},{1,0},{2,3},{3,2},{4,5},{5,4},{6,7},{7,6},{8,9},{9,8},{10,11... | collective-permute-start | bytes 122888 | tf_op jit(solution)/shard_map/ppermute | solution.py:268
  92.4 4.0 %collective-permute-start.20 = (f32[16,640]{1,0:T(8,128)S(1)}, f32[16,640]{1,0:T(8,128)S(1)}, u32[]{:S(2)}, u32[]{:S(2)}) collective-permute-start(f32[16,640]{1,0:T(8,128)S(1)} %add.20), channel_id=1, source_target_pairs={{0,2},{1,3},{2,0},{3,1},{4,6},{5,7},{6,4},{7,5},{8,10},{9,11},{10,... | collective-permute-start | bytes 122888 | tf_op jit(solution)/shard_map/ppermute | solution.py:268
  96.4 5.9 %collective-permute-start.21 = (f32[16,640]{1,0:T(8,128)S(1)}, f32[16,640]{1,0:T(8,128)S(1)}, u32[]{:S(2)}, u32[]{:S(2)}) collective-permute-start(f32[16,640]{1,0:T(8,128)S(1)} %add.21), channel_id=1, source_target_pairs={{0,4},{1,5},{2,6},{3,7},{4,0},{5,1},{6,2},{7,3},{8,12},{9,13},{10,... | collective-permute-start | bytes 122888 | tf_op jit(solution)/shard_map/ppermute | solution.py:268
  115.0 7.5 %collective-permute-start.26 = (bf16[208,512]{1,0:T(8,128)(2,1)}, bf16[208,512]{1,0:T(8,128)(2,1)S(1)}, u32[]{:S(2)}, u32[]{:S(2)}) collective-permute-start(bf16[208,512]{1,0:T(8,128)(2,1)} %get-tuple-element.156), channel_id=1, source_target_pairs={{0,1},{1,0},{2,3},{3,2},{4,5},{5,4},{6,7},{7,6},{8,9},{9,8},{10,11... | collective-permute-start | bytes 638984 | tf_op jit(solution)/shard_map/ppermute | solution.py:268
  116.1 9.5 %collective-permute-start.27 = (bf16[208,512]{1,0:T(8,128)(2,1)}, bf16[208,512]{1,0:T(8,128)(2,1)S(1)}, u32[]{:S(2)}, u32[]{:S(2)}) collective-permute-start(bf16[208,512]{1,0:T(8,128)(2,1)} %get-tuple-element.157), channel_id=1, source_target_pairs={{0,2},{1,3},{2,0},{3,1},{4,6},{5,7},{6,4},{7,5},{8,10},{9,11},{10,... | collective-permute-start | bytes 638984 | tf_op jit(solution)/shard_map/ppermute | solution.py:268
  117.1 24.6 %collective-permute-start.22 = (bf16[208,512]{1,0:T(8,128)(2,1)}, bf16[208,512]{1,0:T(8,128)(2,1)S(1)}, u32[]{:S(2)}, u32[]{:S(2)}) collective-permute-start(bf16[208,512]{1,0:T(8,128)(2,1)} %get-tuple-element.151), channel_id=1, source_target_pairs={{0,4},{1,5},{2,6},{3,7},{4,0},{5,1},{6,2},{7,3},{8,12},{9,13},{10,... | collective-permute-start | bytes 638984 | tf_op jit(solution)/shard_map/ppermute | solution.py:268
  119.4 25.0 %collective-permute-start.23 = (bf16[208,512]{1,0:T(8,128)(2,1)}, bf16[208,512]{1,0:T(8,128)(2,1)S(1)}, u32[]{:S(2)}, u32[]{:S(2)}) collective-permute-start(bf16[208,512]{1,0:T(8,128)(2,1)} %get-tuple-element.152), channel_id=1, source_target_pairs={{0,5},{1,4},{2,7},{3,6},{4,1},{5,0},{6,3},{7,2},{8,13},{9,12},{10,... | collective-permute-start | bytes 638984 | tf_op jit(solution)/shard_map/ppermute | solution.py:268
  120.5 17.7 %collective-permute-start.28 = (bf16[208,512]{1,0:T(8,128)(2,1)}, bf16[208,512]{1,0:T(8,128)(2,1)S(1)}, u32[]{:S(2)}, u32[]{:S(2)}) collective-permute-start(bf16[208,512]{1,0:T(8,128)(2,1)} %get-tuple-element.158), channel_id=1, source_target_pairs={{0,3},{1,2},{2,1},{3,0},{4,7},{5,6},{6,5},{7,4},{8,11},{9,10},{10,... | collective-permute-start | bytes 638984 | tf_op jit(solution)/shard_map/ppermute | solution.py:268
  122.5 27.3 %collective-permute-start.24 = (bf16[208,512]{1,0:T(8,128)(2,1)}, bf16[208,512]{1,0:T(8,128)(2,1)S(1)}, u32[]{:S(2)}, u32[]{:S(2)}) collective-permute-start(bf16[208,512]{1,0:T(8,128)(2,1)} %get-tuple-element.153), channel_id=1, source_target_pairs={{0,6},{1,7},{2,4},{3,5},{4,2},{5,3},{6,0},{7,1},{8,14},{9,15},{10,... | collective-permute-start | bytes 638984 | tf_op jit(solution)/shard_map/ppermute | solution.py:268
  125.7 27.4 %collective-permute-start.25 = (bf16[208,512]{1,0:T(8,128)(2,1)}, bf16[208,512]{1,0:T(8,128)(2,1)S(1)}, u32[]{:S(2)}, u32[]{:S(2)}) collective-permute-start(bf16[208,512]{1,0:T(8,128)(2,1)} %get-tuple-element.154), channel_id=1, source_target_pairs={{0,7},{1,6},{2,5},{3,4},{4,3},{5,2},{6,1},{7,0},{8,15},{9,14},{10,... | collective-permute-start | bytes 638984 | tf_op jit(solution)/shard_map/ppermute | solution.py:268
  (24 other events, 214.2 us)
where the time goes:
time: 157 us
  waiting for transfers between devices  68 us (43%)
  starting transfers between devices  41.6 us (26%)
  Pallas kernels  39.6 us (25%)
  local copies, waits for them, and re-layouts  4 us (3%)
  between operations  1.64 us (1%)
  other arithmetic  1.62 us (1%)
    ppermute x29, waiting for transfers between devices, swap(): return lax.ppermute(value, axis, [(i, i ^ offset) for i in range(size)])  65.7 us
    ppermute x29, starting transfers between devices, swap(): return lax.ppermute(value, axis, [(i, i ^ offset) for i in range(size)])  35.5 us
    pallas_call x2, Pallas kernels, forward(): pl.pallas_call(functools.partial(forward_kernel, plan, piece, 1.0 / all_b...  13.7 us
    pallas_call x1, Pallas kernels, body(): pl.pallas_call(functools.partial(backward_kernel, n, count, tiles_dev, pi...  12.1 us
    all_to_all x1, starting transfers between devices, across(): lax.all_to_all(value, 'grid', split_axis=0, concat_axis=0, tiled=True)  6.12 us
    pallas_call x2, Pallas kernels, body(): pl.pallas_call(functools.partial(unpack_kernel, groups, per, tuple(offset...  5.59 us
    pallas_call x1, Pallas kernels, body(): pl.pallas_call(functools.partial(pack_kernel, groups, per), out_shape=[ja...  3.55 us
  transfers between devices with their start and end apart: 30, of which 20 were waited for; matrix products, arithmetic and copies ran while one was open for 1% of the time, Pallas kernels for 10%

commit v1 on v0

--- a/solution.py
+++ b/solution.py
@@ -151,15 +151,14 @@
 
 
 def tile_blocks(touch_ref, index, blocks):
-    atoms, touch_len = blocks.shape[1], touch_ref.shape[1]
-    ids = [touch_ref[index, s] for s in range(touch_len)]
-    return jnp.concatenate([blocks[a // atoms, a % atoms] for a in ids], axis=0)
-
-
-def tile_basis(beta, index, first, tiles_dev, piece, basis):
-    width, m = basis.shape[:2]
-    slot, column = index % tiles_dev, index // tiles_dev
-    y, k = column % width, column // width
+    return jnp.concatenate(
+        [blocks[touch_ref[index, s]] for s in range(touch_ref.shape[1])], axis=0
+    )
+
+
+def tile_basis(beta, index, y, tiles_dev, piece, basis):
+    m = basis.shape[1]
+    slot, k = index % tiles_dev, index // tiles_dev
     count = m // tiles_dev
     parts = [basis[y, (slot * count + c) ^ beta, k, :piece] for c in range(count)]
     return jnp.concatenate(parts, axis=0), y, k, slot
@@ -174,7 +173,8 @@
     else:
         received, basis_refs = refs[:-4][: -k], refs[:-4][-k:]
         out_ref, blocks, basis, sems = refs[-4:]
-    _, atoms, pad, width = blocks.shape
+    pad, width = blocks.shape[1:]
+    atoms = blocks.shape[0] // n
     copies = load_basis(basis_refs, basis, sems)
     if first:
         copies.append(pltpu.make_async_copy(block_ref, blocks, sems.at[k]))
@@ -187,13 +187,14 @@
             packed = jnp.concatenate([ref[owner] for ref in received], axis=0)
             matrix = matrix[:, : packed.shape[0]]
             value = jnp.dot(matrix, packed, preferred_element_type=jnp.float32)
-            blocks[owner] = value.astype(jnp.bfloat16).reshape(atoms, pad, width)
+            value = value.astype(jnp.bfloat16).reshape(atoms, pad, width)
+            blocks[pl.ds(owner * atoms, atoms)] = value
         out_ref[...] = jnp.zeros_like(out_ref)
     for copy in copies:
         copy.wait()
 
-    def step(index, carry):
-        values, y, z, slot = tile_basis(beta, index, first, tiles_dev, piece, basis)
+    def step(y, index, carry):
+        values, _, z, slot = tile_basis(beta, index, y, tiles_dev, piece, basis)
         d = z * low + first + y
         part = tile_blocks(touch_ref, d * tiles_dev + slot, blocks)
         product = lax.dot_general(
@@ -206,7 +207,8 @@
         )
         return carry
 
-    lax.fori_loop(0, basis.shape[0] * basis.shape[2] * tiles_dev, step, 0, unroll=4)
+    for y in range(basis.shape[0]):
+        lax.fori_loop(0, basis.shape[2] * tiles_dev, functools.partial(step, y), 0, unroll=8)
 
 
 def backward_kernel(
@@ -217,17 +219,17 @@
     spill_ref, blocks, basis, total, sems = refs[k + 1 + n :]
     me, beta = at_ref[0], at_ref[1]
     tile_count, touch_len = touch_ref.shape
-    _, atoms, pad, width = blocks.shape
+    pad, width = blocks.shape[1:]
+    atoms = blocks.shape[0] // n
+    held = pltpu.make_async_copy(block_ref, blocks, sems.at[k])
+    held.start()
     copies = load_basis(basis_refs, basis, sems)
-    copies.append(pltpu.make_async_copy(block_ref, blocks, sems.at[k]))
-    copies[-1].start()
     total[...] = jnp.zeros_like(total)
     weight = weight_ref[...]
-    for copy in copies:
-        copy.wait()
-
-    def step(index, carry):
-        values, y, z, slot = tile_basis(beta, index, 0, tiles_dev, piece, basis)
+    held.wait()
+
+    def step(y, index, carry):
+        values, _, z, slot = tile_basis(beta, index, y, tiles_dev, piece, basis)
         d = z * basis.shape[0] + y
         row = d * tiles_dev + slot
         part = tile_blocks(touch_ref, row, blocks)
@@ -247,7 +249,11 @@
             total[touch_ref[row, s]] += product[s * pad : (s + 1) * pad]
         return carry
 
-    lax.fori_loop(0, tile_count, step, 0, unroll=4)
+    columns, each = basis.shape[0], len(copies) // basis.shape[0]
+    for y in range(columns):
+        for copy in copies[y * each : (y + 1) * each]:
+            copy.wait()
+        lax.fori_loop(0, tile_count // columns, functools.partial(step, y), 0, unroll=4)
     for d, out_ref in enumerate(out_refs):
         owner = me ^ d
         matrix = gather_matrix(lambda a: rows_ref[d, a], atoms, pad)
@@ -395,7 +401,7 @@
         if (y, x, h) not in last:
             pieces[y, x + 1, h] = swap(pieces[y, x, h], "band", 1)
     all_bands = band_dev * m
-    held = jax.ShapeDtypeStruct((n, atoms, pad, width), jnp.bfloat16)
+    held = jax.ShapeDtypeStruct((n * atoms, pad, width), jnp.bfloat16)
     value = jax.ShapeDtypeStruct((tile_count, points), jnp.float32)
     near, far = range(1), range(1, low)
 
@@ -445,7 +451,7 @@
     basis = basis_of(range(low))
     count = len(basis)
     scratch = [
-        pltpu.VMEM((n, atoms, pad, width), jnp.bfloat16),
+        pltpu.VMEM((n * atoms, pad, width), jnp.bfloat16),
         pltpu.VMEM((low, m, n // low, piece + extra, points), jnp.bfloat16),
     ]
     sems = pltpu.SemaphoreType.DMA((1 + count,))
@@ -464,7 +470,9 @@
     returned = exchange(back)
     spill = rest(spill)
     gradient = None
-    for offsets in (range(n // 2), range(n // 2, n)):
+    half = n // 2
+    early = [*range(half - 1), *range(half, n - n // 4), half - 1]
+    for offsets in (early, range(n - n // 4, n)):
         before = [] if gradient is None else [gradient]
         gradient = pl.pallas_call(
             functools.partial(unpack_kernel, groups, per, tuple(offsets)),

time: 157 us -> 155 us (0.987)
  Pallas kernels: 39.6 us -> 37.1 us
where the time goes in v1:
time: 155 us
  waiting for transfers between devices  68.3 us (44%)
  starting transfers between devices  41.7 us (27%)
  Pallas kernels  37.1 us (24%)
  local copies, waits for them, and re-layouts  4.04 us (3%)
  between operations  1.65 us (1%)
  other arithmetic  1.62 us (1%)
    ppermute x29, waiting for transfers between devices, swap(): return lax.ppermute(value, axis, [(i, i ^ offset) for i in range(size)])  65.9 us
    ppermute x29, starting transfers between devices, swap(): return lax.ppermute(value, axis, [(i, i ^ offset) for i in range(size)])  35.6 us
    pallas_call x2, Pallas kernels, forward(): pl.pallas_call(functools.partial(forward_kernel, plan, piece, 1.0 / all_b...  12.2 us
    pallas_call x1, Pallas kernels, body(): pl.pallas_call(functools.partial(backward_kernel, n, count, tiles_dev, pi...  11.1 us
    all_to_all x1, starting transfers between devices, across(): lax.all_to_all(value, 'grid', split_axis=0, concat_axis=0, tiled=True)  6.12 us
    pallas_call x2, Pallas kernels, body(): pl.pallas_call(functools.partial(unpack_kernel, groups, per, tuple(offset...  5.51 us
    pallas_call x1, Pallas kernels, body(): pl.pallas_call(functools.partial(pack_kernel, groups, per), out_shape=[ja...  3.55 us
  transfers between devices with their start and end apart: 30, of which 20 were waited for; matrix products, arithmetic and copies ran while one was open for 1% of the time, Pallas kernels for 10%

profile of v1, /device:TPU:8, one launch (start us, length us, event | category | flops | bytes accessed | tf_op | source)
XLA Modules:
  0.0 154.6 jit_solution(332252523997912672)
XLA Ops:
  8.0 3.5 %pack.1 = (bf16[8,208,512]{2,1,0:T(8,128)(2,1)}, bf16[8,48,512]{2,1,0:T(8,128)(2,1)}) custom-call(s32[16]{0:T(128)} %rows_ref.5, bf16[16,16,3840]{2,1,0:T(8,128)(2,1)} %coef_ref.1), custom_call_target="tpu_custom_call" | custom-call | tf_op jit(solution)/shard_map/pack/pallas_call | solution.py:339
  11.6 7.4 %collective-permute-done.2 = bf16[144,640]{1,0:T(8,128)(2,1)S(1)} collective-permute-done((bf16[144,640]{1,0:T(8,128)(2,1)S(1)}, bf16[144,640]{1,0:T(8,128)(2,1)S(1)}, u32[]{:S(2)}, u32[]{:S(2)}) %collective-permute-start.2) | collective-permute-done | bytes 184352 | tf_op jit(solution)/shard_map/ppermute | solution.py:274
  19.0 2.0 %collective-permute-done.1 = bf16[144,640]{1,0:T(8,128)(2,1)S(1)} collective-permute-done((bf16[144,640]{1,0:T(8,128)(2,1)S(1)}, bf16[144,640]{1,0:T(8,128)(2,1)S(1)}, u32[]{:S(2)}, u32[]{:S(2)}) %collective-permute-start.1) | collective-permute-done | bytes 184352 | tf_op jit(solution)/shard_map/ppermute | solution.py:274
  21.0 6.1 %all-to-all-start.2 = ((bf16[8,208,512]{2,1,0:T(8,128)(2,1)}), bf16[8,208,512]{2,1,0:T(8,128)(2,1)S(1)}, u32[]{:S(2)}, u32[]{:S(2)}) async-start(bf16[8,208,512]{2,1,0:T(8,128)(2,1)} %get-tuple-element.138), calls=%async_computation.2 | async-start | bytes 3407872 | tf_op jit(solution)/shard_map/all_to_all | solution.py:309
  35.2 12.2 %collective-permute-done.4.refs_5_.refs_4_ = bf16[1,144,640]{2,1,0:T(8,128)(2,1)S(1)} collective-permute-done((bf16[1,144,640]{2,1,0:T(8,128)(2,1)S(1)}, bf16[1,144,640]{2,1,0:T(8,128)(2,1)S(1)}, u32[]{:S(2)}, u32[]{:S(2)}) %collective-permute-start.4) | collective-permute-done | bytes 184352 | tf_op jit(solution)/shard_map/ppermute | solution.py:274
  49.4 7.0 %collective-permute-done.6.refs_3_.refs_9_ = bf16[3,144,640]{2,1,0:T(8,128)(2,1)S(1)} collective-permute-done((bf16[3,144,640]{2,1,0:T(8,128)(2,1)S(1)}, bf16[3,144,640]{2,1,0:T(8,128)(2,1)S(1)}, u32[]{:S(2)}, u32[]{:S(2)}) %collective-permute-start.6) | collective-permute-done | bytes 552992 | tf_op jit(solution)/shard_map/ppermute | solution.py:274
  60.6 2.3 %all-to-all-done.2.refs_0_ = bf16[8,208,512]{2,1,0:T(8,128)(2,1)S(1)} async-done(((bf16[8,208,512]{2,1,0:T(8,128)(2,1)}), bf16[8,208,512]{2,1,0:T(8,128)(2,1)S(1)}, u32[]{:S(2)}, u32[]{:S(2)}) %all-to-all-start.2) | async-done | bytes 1703968 | tf_op jit(solution)/shard_map/all_to_all | solution.py:309
  62.9 6.1 %forward.6 = (f32[16,640]{1,0:T(8,128)}, bf16[128,16,512]{2,1,0:T(8,128)(2,1)}) custom-call(s32[16,16]{1,0:T(8,128)S(1)} %get-tuple-element.133.touch_ref, s32[8,16]{1,0:T(8,128)} %get-tuple-element.134.rows_ref, s32[2]{0:T(128)} %copy-done.15, f32[512,128]{1,0:T(8,128)} %get-tuple-element.137.weight_ref, bf16[8,208,512]{2,1,0:T(8,128)(2,1)S(1)} %all-to-all-done.2.refs_0_, ...), custom_call_target="tpu_custom_call" | custom-call | flops 1342177280 | bytes 134217728 | tf_op jit(solution)/shard_map/forward/pallas_call | solution.py:420
  69.0 2.5 %collective-permute-done.8.refs_7_.refs_13_ = bf16[3,144,640]{2,1,0:T(8,128)(2,1)S(1)} collective-permute-done((bf16[3,144,640]{2,1,0:T(8,128)(2,1)S(1)}, bf16[3,144,640]{2,1,0:T(8,128)(2,1)S(1)}, u32[]{:S(2)}, u32[]{:S(2)}) %collective-permute-start.8) | collective-permute-done | bytes 552992 | tf_op jit(solution)/shard_map/ppermute | solution.py:274
  74.6 6.0 %forward.7 = f32[16,640]{1,0:T(8,128)} custom-call(s32[16,16]{1,0:T(8,128)S(1)} %get-tuple-element.133.touch_ref, s32[8,16]{1,0:T(8,128)S(1)} %copy-done.14, s32[2]{0:T(128)S(1)} %copy-done.16, f32[512,128]{1,0:T(8,128)} %get-tuple-element.137.weight_ref, f32[16,640]{1,0:T(8,128)} %get-tuple-element.143.refs_0_, ...), custom_call_target="tpu_custom_call" | custom-call | flops 1342177280 | bytes 134217728 | tf_op jit(solution)/shard_map/forward/pallas_call | solution.py:420
  84.7 2.5 %collective-permute-done.18 = f32[16,640]{1,0:T(8,128)S(1)} collective-permute-done((f32[16,640]{1,0:T(8,128)S(1)}, f32[16,640]{1,0:T(8,128)S(1)}, u32[]{:S(2)}, u32[]{:S(2)}) %collective-permute-start.18) | collective-permute-done | bytes 40992 | tf_op jit(solution)/shard_map/ppermute | solution.py:274
  87.2 2.5 %collective-permute-start.19 = (f32[16,640]{1,0:T(8,128)S(1)}, f32[16,640]{1,0:T(8,128)S(1)}, u32[]{:S(2)}, u32[]{:S(2)}) collective-permute-start(f32[16,640]{1,0:T(8,128)S(1)} %add.19), channel_id=1, source_target_pairs={{0,1},{1,0},{2,3},{3,2},{4,5},{5,4},{6,7},{7,6},{8,9},{9,8},{10,11... | collective-permute-start | bytes 122888 | tf_op jit(solution)/shard_map/ppermute | solution.py:274
  91.7 2.0 %collective-permute-start.20 = (f32[16,640]{1,0:T(8,128)S(1)}, f32[16,640]{1,0:T(8,128)S(1)}, u32[]{:S(2)}, u32[]{:S(2)}) collective-permute-start(f32[16,640]{1,0:T(8,128)S(1)} %add.20), channel_id=1, source_target_pairs={{0,2},{1,3},{2,0},{3,1},{4,6},{5,7},{6,4},{7,5},{8,10},{9,11},{10,... | collective-permute-start | bytes 122888 | tf_op jit(solution)/shard_map/ppermute | solution.py:274
  95.7 3.9 %collective-permute-start.21 = (f32[16,640]{1,0:T(8,128)S(1)}, f32[16,640]{1,0:T(8,128)S(1)}, u32[]{:S(2)}, u32[]{:S(2)}) collective-permute-start(f32[16,640]{1,0:T(8,128)S(1)} %add.21), channel_id=1, source_target_pairs={{0,4},{1,5},{2,6},{3,7},{4,0},{5,1},{6,2},{7,3},{8,12},{9,13},{10,... | collective-permute-start | bytes 122888 | tf_op jit(solution)/shard_map/ppermute | solution.py:274
  99.6 2.0 %collective-permute-done.21 = f32[16,640]{1,0:T(8,128)S(1)} collective-permute-done((f32[16,640]{1,0:T(8,128)S(1)}, f32[16,640]{1,0:T(8,128)S(1)}, u32[]{:S(2)}, u32[]{:S(2)}) %collective-permute-start.21) | collective-permute-done | bytes 40992 | tf_op jit(solution)/shard_map/ppermute | solution.py:274
  102.3 11.1 %backward.1 = (bf16[208,512]{1,0:T(8,128)(2,1)}, bf16[208,512]{1,0:T(8,128)(2,1)}, bf16[208,512]{1,0:T(8,128)(2,1)}, bf16[208,512]{1,0:T(8,128)(2,1)}, bf16[208,...) custom-call(s32[16,16]{1,0:T(8,128)S(1)} %get-tuple-element.133.touc, ...), custom_call_target="tpu_custom_call" | custom-call | tf_op jit(solution)/shard_map/backward/pallas_call | solution.py:460
  114.9 2.9 %collective-permute-start.26 = (bf16[208,512]{1,0:T(8,128)(2,1)}, bf16[208,512]{1,0:T(8,128)(2,1)S(1)}, u32[]{:S(2)}, u32[]{:S(2)}) collective-permute-start(bf16[208,512]{1,0:T(8,128)(2,1)} %get-tuple-element.156), channel_id=1, source_target_pairs={{0,4},{1,5},{2,6},{3,7},{4,0},{5,1},{6,2},{7,3},{8,12},{9,13},{10,... | collective-permute-start | bytes 638984 | tf_op jit(solution)/shard_map/ppermute | solution.py:274
  120.9 2.4 %collective-permute-start.22 = (bf16[208,512]{1,0:T(8,128)(2,1)}, bf16[208,512]{1,0:T(8,128)(2,1)S(1)}, u32[]{:S(2)}, u32[]{:S(2)}) collective-permute-start(bf16[208,512]{1,0:T(8,128)(2,1)} %get-tuple-element.151), channel_id=1, source_target_pairs={{0,6},{1,7},{2,4},{3,5},{4,2},{5,3},{6,0},{7,1},{8,14},{9,15},{10,... | collective-permute-start | bytes 638984 | tf_op jit(solution)/shard_map/ppermute | solution.py:274
  124.0 2.3 %collective-permute-start.23 = (bf16[208,512]{1,0:T(8,128)(2,1)}, bf16[208,512]{1,0:T(8,128)(2,1)S(1)}, u32[]{:S(2)}, u32[]{:S(2)}) collective-permute-start(bf16[208,512]{1,0:T(8,128)(2,1)} %get-tuple-element.152), channel_id=1, source_target_pairs={{0,7},{1,6},{2,5},{3,4},{4,3},{5,2},{6,1},{7,0},{8,15},{9,14},{10,... | collective-permute-start | bytes 638984 | tf_op jit(solution)/shard_map/ppermute | solution.py:274
  126.9 5.6 %collective-permute-done.26.refs_3_ = bf16[208,512]{1,0:T(8,128)(2,1)S(1)} collective-permute-done((bf16[208,512]{1,0:T(8,128)(2,1)}, bf16[208,512]{1,0:T(8,128)(2,1)S(1)}, u32[]{:S(2)}, u32[]{:S(2)}) %collective-permute-start.26) | collective-permute-done | bytes 213024 | tf_op jit(solution)/shard_map/ppermute | solution.py:274
  132.5 10.3 %collective-permute-done.27.refs_4_ = bf16[208,512]{1,0:T(8,128)(2,1)S(1)} collective-permute-done((bf16[208,512]{1,0:T(8,128)(2,1)}, bf16[208,512]{1,0:T(8,128)(2,1)S(1)}, u32[]{:S(2)}, u32[]{:S(2)}) %collective-permute-start.27) | collective-permute-done | bytes 213024 | tf_op jit(solution)/shard_map/ppermute | solution.py:274
  143.6 3.2 %unpack.2.refs_2_ = f32[16,16,3840]{2,1,0:T(8,128)} custom-call(s32[16]{0:T(128)} %rows_ref.5, s32[2]{0:T(128)S(1)} %copy-done.17, bf16[8,48,512]{2,1,0:T(8,128)(2,1)S(1)} %get-tuple-element.166.spill_ref, bf16[208,512]{1,0:T(8,128)(2,1)} %get-tuple-element.153.refs_0_, bf16[208,512]{1,0:T(8,128)(2,1)} %copy-done.7, bf16[208,512]{1,0:T(8,128)(2,1)} %copy-done.8, ...), custom_call_target="tpu_custom_call" | custom-call | bytes 4194304 | tf_op jit(solution)/shard_map/unpack/pallas_call | solution.py:477
  148.2 3.3 %collective-permute-done.23.refs_1_ = bf16[208,512]{1,0:T(8,128)(2,1)S(1)} collective-permute-done((bf16[208,512]{1,0:T(8,128)(2,1)}, bf16[208,512]{1,0:T(8,128)(2,1)S(1)}, u32[]{:S(2)}, u32[]{:S(2)}) %collective-permute-start.23) | collective-permute-done | bytes 213024 | tf_op jit(solution)/shard_map/ppermute | solution.py:274
  152.1 2.3 %unpack.3 = f32[16,16,3840]{2,1,0:T(8,128)} custom-call(s32[16]{0:T(128)} %rows_ref.5, s32[2]{0:T(128)S(1)} %copy-done.17, bf16[8,48,512]{2,1,0:T(8,128)(2,1)S(1)} %get-tuple-element.166.spill_ref, bf16[208,512]{1,0:T(8,128)(2,1)} %copy-done.11, bf16[208,512]{1,0:T(8,128)(2,1)} %copy-done.13, ...), custom_call_target="tpu_custom_call", output_to_operand_aliasing={{}: (5, {})} | custom-call | bytes 4194304 | tf_op jit(solution)/shard_map/unpack/pallas_call | solution.py:477
  (92 shorter events, 41.3 us)
Async XLA Ops:
  2.4 9.2 %collective-permute-start.3 = (bf16[1,144,640]{2,1,0:T(8,128)(2,1)S(1)}, bf16[1,144,640]{2,1,0:T(8,128)(2,1)S(1)}, u32[]{:S(2)}, u32[]{:S(2)}) collective-permute-start(bf16[1,144,640]{2,1,0:T(8,128)(2,1)S(1)} %bitcast.9), channel_id=1, source_target_pairs={{0,1},{1,0},{2,3},{3,2},{4,5},{5,4},{6,7},{7,6},{8,9},{9,8},{10,11... | collective-permute-start | bytes 552968 | tf_op jit(solution)/shard_map/ppermute | solution.py:274
  4.0 15.0 %collective-permute-start.2 = (bf16[144,640]{1,0:T(8,128)(2,1)S(1)}, bf16[144,640]{1,0:T(8,128)(2,1)S(1)}, u32[]{:S(2)}, u32[]{:S(2)}) collective-permute-start(bf16[144,640]{1,0:T(8,128)(2,1)S(1)} %prep.1), channel_id=1, source_target_pairs={{0,6},{1,7},{2,4},{3,5},{4,2},{5,3},{6,0},{7,1},{8,14},{9,15},{10,... | collective-permute-start | bytes 552968 | tf_op jit(solution)/shard_map/ppermute | solution.py:274
  5.6 15.5 %collective-permute-start.1 = (bf16[144,640]{1,0:T(8,128)(2,1)S(1)}, bf16[144,640]{1,0:T(8,128)(2,1)S(1)}, u32[]{:S(2)}, u32[]{:S(2)}) collective-permute-start(bf16[144,640]{1,0:T(8,128)(2,1)S(1)} %prep.1), channel_id=1, source_target_pairs={{0,4},{1,5},{2,6},{3,7},{4,0},{5,1},{6,2},{7,3},{8,12},{9,13},{10,... | collective-permute-start | bytes 552968 | tf_op jit(solution)/shard_map/ppermute | solution.py:274
  6.8 14.2 %collective-permute-start = (bf16[144,640]{1,0:T(8,128)(2,1)S(1)}, bf16[144,640]{1,0:T(8,128)(2,1)S(1)}, u32[]{:S(2)}, u32[]{:S(2)}) collective-permute-start(bf16[144,640]{1,0:T(8,128)(2,1)S(1)} %prep.1), channel_id=1, source_target_pairs={{0,2},{1,3},{2,0},{3,1},{4,6},{5,7},{6,4},{7,5},{8,10},{9,11},{10,... | collective-permute-start | bytes 552968 | tf_op jit(solution)/shard_map/ppermute | solution.py:274
  21.0 41.8 %all-to-all-start.2 = ((bf16[8,208,512]{2,1,0:T(8,128)(2,1)}), bf16[8,208,512]{2,1,0:T(8,128)(2,1)S(1)}, u32[]{:S(2)}, u32[]{:S(2)}) async-start(bf16[8,208,512]{2,1,0:T(8,128)(2,1)} %get-tuple-element.138), calls=%async_computation.2 | async-start | bytes 3407872 | tf_op jit(solution)/shard_map/all_to_all | solution.py:309
  27.2 29.2 %collective-permute-start.6 = (bf16[3,144,640]{2,1,0:T(8,128)(2,1)S(1)}, bf16[3,144,640]{2,1,0:T(8,128)(2,1)S(1)}, u32[]{:S(2)}, u32[]{:S(2)}) collective-permute-start(bf16[3,144,640]{2,1,0:T(8,128)(2,1)S(1)} %pad_maximum_fusion.after_ref.refs_1_.refs_2_), channel_id=1, source_target_pairs={{0,1},{1,0},{2,3},{3,2},{4,5},{5,4},{6,7},{7,6},{8,9},{9,8},{10,11... | collective-permute-start | bytes 1658888 | tf_op jit(solution)/shard_map/ppermute | solution.py:274
  28.7 27.7 %collective-permute-start.5 = (bf16[3,144,640]{2,1,0:T(8,128)(2,1)S(1)}, bf16[3,144,640]{2,1,0:T(8,128)(2,1)S(1)}, u32[]{:S(2)}, u32[]{:S(2)}) collective-permute-start(bf16[3,144,640]{2,1,0:T(8,128)(2,1)S(1)} %pad_maximum_fusion.after_ref.refs_1_.refs_2_), channel_id=1, source_target_pairs={{0,16},{8,24},{16,0},{24,8},{1,17},{9,25},{17,1},{25,9},{2,18},{10... | collective-permute-start | bytes 1658888 | tf_op jit(solution)/shard_map/ppermute | solution.py:274
  30.2 17.2 %collective-permute-start.4 = (bf16[1,144,640]{2,1,0:T(8,128)(2,1)S(1)}, bf16[1,144,640]{2,1,0:T(8,128)(2,1)S(1)}, u32[]{:S(2)}, u32[]{:S(2)}) collective-permute-start(bf16[1,144,640]{2,1,0:T(8,128)(2,1)S(1)} %bitcast.10), channel_id=1, source_target_pairs={{0,16},{8,24},{16,0},{24,8},{1,17},{9,25},{17,1},{25,9},{2,18},{10... | collective-permute-start | bytes 552968 | tf_op jit(solution)/shard_map/ppermute | solution.py:274
  30.8 18.6 %collective-permute-start.7 = (bf16[1,144,640]{2,1,0:T(8,128)(2,1)S(1)}, bf16[1,144,640]{2,1,0:T(8,128)(2,1)S(1)}, u32[]{:S(2)}, u32[]{:S(2)}) collective-permute-start(bf16[1,144,640]{2,1,0:T(8,128)(2,1)S(1)} %collective-permute-done.3.refs_2_.refs_8_), channel_id=1, source_target_pairs={{0,16},{8,24},{16,0},{24,8},{1,17},{9,25},{17,1},{25,9},{2,18},{10... | collective-permute-start | bytes 552968 | tf_op jit(solution)/shard_map/ppermute | solution.py:274
  56.4 4.1 %collective-permute-start.12 = (bf16[3,144,640]{2,1,0:T(8,128)(2,1)S(1)}, bf16[3,144,640]{2,1,0:T(8,128)(2,1)}, u32[]{:S(2)}, u32[]{:S(2)}) collective-permute-start(bf16[3,144,640]{2,1,0:T(8,128)(2,1)S(1)} %collective-permute-done.5.refs_6_.refs_5_), channel_id=1, source_target_pairs={{0,8},{8,0},{16,24},{24,16},{1,9},{9,1},{17,25},{25,17},{2,10},{10... | collective-permute-start | bytes 1658888 | tf_op jit(solution)/shard_map/ppermute | solution.py:274
  56.5 4.1 %collective-permute-start.10 = (bf16[3,144,640]{2,1,0:T(8,128)(2,1)S(1)}, bf16[3,144,640]{2,1,0:T(8,128)(2,1)}, u32[]{:S(2)}, u32[]{:S(2)}) collective-permute-start(bf16[3,144,640]{2,1,0:T(8,128)(2,1)S(1)} %pad_maximum_fusion.after_ref.refs_1_.refs_2_), channel_id=1, source_target_pairs={{0,8},{8,0},{16,24},{24,16},{1,9},{9,1},{17,25},{25,17},{2,10},{10... | collective-permute-start | bytes 1658888 | tf_op jit(solution)/shard_map/ppermute | solution.py:274
  57.0 14.5 %collective-permute-start.8 = (bf16[3,144,640]{2,1,0:T(8,128)(2,1)S(1)}, bf16[3,144,640]{2,1,0:T(8,128)(2,1)S(1)}, u32[]{:S(2)}, u32[]{:S(2)}) collective-permute-start(bf16[3,144,640]{2,1,0:T(8,128)(2,1)S(1)} %collective-permute-done.6.refs_3_.refs_9_), channel_id=1, source_target_pairs={{0,16},{8,24},{16,0},{24,8},{1,17},{9,25},{17,1},{25,9},{2,18},{10... | collective-permute-start | bytes 1658888 | tf_op jit(solution)/shard_map/ppermute | solution.py:274
  60.4 13.5 %collective-permute-start.14 = (bf16[3,144,640]{2,1,0:T(8,128)(2,1)S(1)}, bf16[3,144,640]{2,1,0:T(8,128)(2,1)}, u32[]{:S(2)}, u32[]{:S(2)}) collective-permute-start(bf16[3,144,640]{2,1,0:T(8,128)(2,1)S(1)} %collective-permute-done.6.refs_3_.refs_9_), channel_id=1, source_target_pairs={{0,8},{8,0},{16,24},{24,16},{1,9},{9,1},{17,25},{25,17},{2,10},{10... | collective-permute-start | bytes 1658888 | tf_op jit(solution)/shard_map/ppermute | solution.py:274
  83.2 4.0 %collective-permute-start.18 = (f32[16,640]{1,0:T(8,128)S(1)}, f32[16,640]{1,0:T(8,128)S(1)}, u32[]{:S(2)}, u32[]{:S(2)}) collective-permute-start(f32[16,640]{1,0:T(8,128)S(1)} %add.18), channel_id=1, source_target_pairs={{0,16},{8,24},{16,0},{24,8},{1,17},{9,25},{17,1},{25,9},{2,18},{10... | collective-permute-start | bytes 122888 | tf_op jit(solution)/shard_map/ppermute | solution.py:274
  87.2 4.5 %collective-permute-start.19 = (f32[16,640]{1,0:T(8,128)S(1)}, f32[16,640]{1,0:T(8,128)S(1)}, u32[]{:S(2)}, u32[]{:S(2)}) collective-permute-start(f32[16,640]{1,0:T(8,128)S(1)} %add.19), channel_id=1, source_target_pairs={{0,1},{1,0},{2,3},{3,2},{4,5},{5,4},{6,7},{7,6},{8,9},{9,8},{10,11... | collective-permute-start | bytes 122888 | tf_op jit(solution)/shard_map/ppermute | solution.py:274
  91.7 4.0 %collective-permute-start.20 = (f32[16,640]{1,0:T(8,128)S(1)}, f32[16,640]{1,0:T(8,128)S(1)}, u32[]{:S(2)}, u32[]{:S(2)}) collective-permute-start(f32[16,640]{1,0:T(8,128)S(1)} %add.20), channel_id=1, source_target_pairs={{0,2},{1,3},{2,0},{3,1},{4,6},{5,7},{6,4},{7,5},{8,10},{9,11},{10,... | collective-permute-start | bytes 122888 | tf_op jit(solution)/shard_map/ppermute | solution.py:274
  95.7 5.9 %collective-permute-start.21 = (f32[16,640]{1,0:T(8,128)S(1)}, f32[16,640]{1,0:T(8,128)S(1)}, u32[]{:S(2)}, u32[]{:S(2)}) collective-permute-start(f32[16,640]{1,0:T(8,128)S(1)} %add.21), channel_id=1, source_target_pairs={{0,4},{1,5},{2,6},{3,7},{4,0},{5,1},{6,2},{7,3},{8,12},{9,13},{10,... | collective-permute-start | bytes 122888 | tf_op jit(solution)/shard_map/ppermute | solution.py:274
  113.4 7.5 %collective-permute-start.24 = (bf16[208,512]{1,0:T(8,128)(2,1)}, bf16[208,512]{1,0:T(8,128)(2,1)S(1)}, u32[]{:S(2)}, u32[]{:S(2)}) collective-permute-start(bf16[208,512]{1,0:T(8,128)(2,1)} %get-tuple-element.154), channel_id=1, source_target_pairs={{0,1},{1,0},{2,3},{3,2},{4,5},{5,4},{6,7},{7,6},{8,9},{9,8},{10,11... | collective-permute-start | bytes 638984 | tf_op jit(solution)/shard_map/ppermute | solution.py:274
  114.5 9.5 %collective-permute-start.25 = (bf16[208,512]{1,0:T(8,128)(2,1)}, bf16[208,512]{1,0:T(8,128)(2,1)S(1)}, u32[]{:S(2)}, u32[]{:S(2)}) collective-permute-start(bf16[208,512]{1,0:T(8,128)(2,1)} %get-tuple-element.155), channel_id=1, source_target_pairs={{0,2},{1,3},{2,0},{3,1},{4,6},{5,7},{6,4},{7,5},{8,10},{9,11},{10,... | collective-permute-start | bytes 638984 | tf_op jit(solution)/shard_map/ppermute | solution.py:274
  114.9 17.7 %collective-permute-start.26 = (bf16[208,512]{1,0:T(8,128)(2,1)}, bf16[208,512]{1,0:T(8,128)(2,1)S(1)}, u32[]{:S(2)}, u32[]{:S(2)}) collective-permute-start(bf16[208,512]{1,0:T(8,128)(2,1)} %get-tuple-element.156), channel_id=1, source_target_pairs={{0,4},{1,5},{2,6},{3,7},{4,0},{5,1},{6,2},{7,3},{8,12},{9,13},{10,... | collective-permute-start | bytes 638984 | tf_op jit(solution)/shard_map/ppermute | solution.py:274
  117.8 25.0 %collective-permute-start.27 = (bf16[208,512]{1,0:T(8,128)(2,1)}, bf16[208,512]{1,0:T(8,128)(2,1)S(1)}, u32[]{:S(2)}, u32[]{:S(2)}) collective-permute-start(bf16[208,512]{1,0:T(8,128)(2,1)} %get-tuple-element.157), channel_id=1, source_target_pairs={{0,5},{1,4},{2,7},{3,6},{4,1},{5,0},{6,3},{7,2},{8,13},{9,12},{10,... | collective-permute-start | bytes 638984 | tf_op jit(solution)/shard_map/ppermute | solution.py:274
  118.9 23.9 %collective-permute-start.28 = (bf16[208,512]{1,0:T(8,128)(2,1)}, bf16[208,512]{1,0:T(8,128)(2,1)S(1)}, u32[]{:S(2)}, u32[]{:S(2)}) collective-permute-start(bf16[208,512]{1,0:T(8,128)(2,1)} %get-tuple-element.158), channel_id=1, source_target_pairs={{0,3},{1,2},{2,1},{3,0},{4,7},{5,6},{6,5},{7,4},{8,11},{9,10},{10,... | collective-permute-start | bytes 638984 | tf_op jit(solution)/shard_map/ppermute | solution.py:274
  120.9 27.3 %collective-permute-start.22 = (bf16[208,512]{1,0:T(8,128)(2,1)}, bf16[208,512]{1,0:T(8,128)(2,1)S(1)}, u32[]{:S(2)}, u32[]{:S(2)}) collective-permute-start(bf16[208,512]{1,0:T(8,128)(2,1)} %get-tuple-element.151), channel_id=1, source_target_pairs={{0,6},{1,7},{2,4},{3,5},{4,2},{5,3},{6,0},{7,1},{8,14},{9,15},{10,... | collective-permute-start | bytes 638984 | tf_op jit(solution)/shard_map/ppermute | solution.py:274
  124.0 27.4 %collective-permute-start.23 = (bf16[208,512]{1,0:T(8,128)(2,1)}, bf16[208,512]{1,0:T(8,128)(2,1)S(1)}, u32[]{:S(2)}, u32[]{:S(2)}) collective-permute-start(bf16[208,512]{1,0:T(8,128)(2,1)} %get-tuple-element.152), channel_id=1, source_target_pairs={{0,7},{1,6},{2,5},{3,4},{4,3},{5,2},{6,1},{7,0},{8,15},{9,14},{10,... | collective-permute-start | bytes 638984 | tf_op jit(solution)/shard_map/ppermute | solution.py:274
  (24 other events, 222.6 us)

commit v2 on v1

--- a/solution.py
+++ b/solution.py
@@ -138,11 +138,10 @@
     more_ref[...] = (most > keep).astype(jnp.int32)
 
 
-def load_basis(basis_refs, basis, sems):
-    m = basis.shape[1]
+def load_basis(keys, basis_refs, basis, sems):
     copies = []
     for index, ref in enumerate(basis_refs):
-        part, y, e = index % 2, index // 2 // m, index // 2 % m
+        part, (y, e) = index % 2, keys[index // 2]
         target = basis.at[y, e, part : part + ref.shape[0]]
         copies.append(pltpu.make_async_copy(ref, target, sems.at[index]))
     for copy in copies:
@@ -156,16 +155,15 @@
     )
 
 
-def tile_basis(beta, index, y, tiles_dev, piece, basis):
-    m = basis.shape[1]
-    slot, k = index % tiles_dev, index // tiles_dev
-    count = m // tiles_dev
+def tile_basis(beta, y, k, slot, tiles_dev, piece, basis):
+    count = basis.shape[1] // tiles_dev
     parts = [basis[y, (slot * count + c) ^ beta, k, :piece] for c in range(count)]
-    return jnp.concatenate(parts, axis=0), y, k, slot
+    return jnp.concatenate(parts, axis=0)
 
 
 def forward_kernel(plan, piece, scale, touch_ref, rows_ref, at_ref, weight_ref, *refs):
-    n, k, low, tiles_dev, first = plan
+    n, keys, tiles_dev, first = plan
+    k = 2 * len(keys)
     me, beta = at_ref[0], at_ref[1]
     if first:
         before_ref, block_ref, basis_refs = refs[0], refs[1], refs[2 : 2 + k]
@@ -175,7 +173,7 @@
         out_ref, blocks, basis, sems = refs[-4:]
     pad, width = blocks.shape[1:]
     atoms = blocks.shape[0] // n
-    copies = load_basis(basis_refs, basis, sems)
+    copies = load_basis(keys, basis_refs, basis, sems)
     if first:
         copies.append(pltpu.make_async_copy(block_ref, blocks, sems.at[k]))
         copies[-1].start()
@@ -193,9 +191,16 @@
     for copy in copies:
         copy.wait()
 
-    def step(y, index, carry):
-        values, _, z, slot = tile_basis(beta, index, y, tiles_dev, piece, basis)
-        d = z * low + first + y
+    low, m, size = basis.shape[:3]
+    own = beta // (m // tiles_dev)
+
+    def step(y, slots, index, carry):
+        z, slot = index // len(slots), slots[0]
+        if len(slots) > 1:
+            slot = slots[0] + index % len(slots)
+        slot = (slot + own) % tiles_dev
+        values = tile_basis(beta, y, z, slot, tiles_dev, piece, basis)
+        d = z * low + y
         part = tile_blocks(touch_ref, d * tiles_dev + slot, blocks)
         product = lax.dot_general(
             part, values, (((0,), (0,)), ((), ())), preferred_element_type=jnp.float32
@@ -207,8 +212,12 @@
         )
         return carry
 
-    for y in range(basis.shape[0]):
-        lax.fori_loop(0, basis.shape[2] * tiles_dev, functools.partial(step, y), 0, unroll=8)
+    for y in range(1 if first else 0, low):
+        slots = range(1, tiles_dev) if first else range(tiles_dev if y == 0 else 1)
+        if slots:
+            lax.fori_loop(
+                0, size * len(slots), functools.partial(step, y, slots), 0, unroll=4
+            )
 
 
 def backward_kernel(
@@ -223,13 +232,15 @@
     atoms = blocks.shape[0] // n
     held = pltpu.make_async_copy(block_ref, blocks, sems.at[k])
     held.start()
-    copies = load_basis(basis_refs, basis, sems)
+    keys = [(y, e) for y in range(basis.shape[0]) for e in range(basis.shape[1])]
+    copies = load_basis(keys, basis_refs, basis, sems)
     total[...] = jnp.zeros_like(total)
     weight = weight_ref[...]
     held.wait()
 
     def step(y, index, carry):
-        values, _, z, slot = tile_basis(beta, index, y, tiles_dev, piece, basis)
+        z, slot = index // tiles_dev, index % tiles_dev
+        values = tile_basis(beta, y, z, slot, tiles_dev, piece, basis)
         d = z * basis.shape[0] + y
         row = d * tiles_dev + slot
         part = tile_blocks(touch_ref, row, blocks)
@@ -253,7 +264,7 @@
     for y in range(columns):
         for copy in copies[y * each : (y + 1) * each]:
             copy.wait()
-        lax.fori_loop(0, tile_count // columns, functools.partial(step, y), 0, unroll=4)
+        lax.fori_loop(0, tile_count // columns, functools.partial(step, y), 0, unroll=8)
     for d, out_ref in enumerate(out_refs):
         owner = me ^ d
         matrix = gather_matrix(lambda a: rows_ref[d, a], atoms, pad)
@@ -365,7 +376,8 @@
         cost_estimate=cover,
         name="weights",
     )(at, occupations[None, :], pieces[0, 0, 1])
-    last = [(y, x, 1) for y in range(1, low) for x in range(2, m, 2)]
+    count = m // tiles_dev
+    last = [(y, x, 1) for y in range(1, low) for x in range(max(2, count), m, 2)]
     for h in parts:
         for y in range(low):
             for x in range(2, m, 2):
@@ -403,17 +415,19 @@
     all_bands = band_dev * m
     held = jax.ShapeDtypeStruct((n * atoms, pad, width), jnp.bfloat16)
     value = jax.ShapeDtypeStruct((tile_count, points), jnp.float32)
-    near, far = range(1), range(1, low)
-
-    def basis_of(columns):
-        return [pieces[y, e, h] for y in columns for e in range(m) for h in parts]
-
-    def forward(columns, inputs):
-        arrays = basis_of(columns)
-        first = columns[0]
-        plan = (n, len(arrays), low, tiles_dev, first)
+    every = [(y, e) for y in range(low) for e in range(m)]
+    far = [(y, e) for y, e in every if y > 0 and e >= count]
+    near = [key for key in every if key not in far]
+
+    def basis_of(keys):
+        return [pieces[y, e, h] for y, e in keys for h in parts]
+
+    def forward(keys, inputs):
+        arrays = basis_of(keys)
+        first = keys is far
+        plan = (n, keys, tiles_dev, first)
         room = [
-            pltpu.VMEM((len(columns), m, size, piece + extra, points), jnp.bfloat16),
+            pltpu.VMEM((low, m, size, piece + extra, points), jnp.bfloat16),
             pltpu.SemaphoreType.DMA((1 + len(arrays),)),
         ]
         places = [vmem, anywhere] if first else [vmem] * len(inputs)
@@ -422,10 +436,10 @@
             out_shape=value if first else [value, held],
             in_specs=[smem, smem, smem, vmem] + places + [anywhere] * len(arrays),
             out_specs=vmem if first else [vmem, vmem],
-            scratch_shapes=[pltpu.VMEM(held.shape, held.dtype)] * (first > 0) + room,
+            scratch_shapes=[pltpu.VMEM(held.shape, held.dtype)] * first + room,
             compiler_params=params,
             cost_estimate=pl.CostEstimate(
-                flops=2 * tile_count // low * len(columns) * slots * width * points,
+                flops=2 * tile_count * len(keys) // len(every) * slots * width * points,
                 bytes_accessed=1 << 27,
                 transcendentals=0,
             ),
@@ -448,7 +462,7 @@
     partial_value, blocks = lax.cond(
         more, again, lambda spill, *same: same, spill, partial_value, blocks
     )
-    basis = basis_of(range(low))
+    basis = basis_of(every)
     count = len(basis)
     scratch = [
         pltpu.VMEM((n * atoms, pad, width), jnp.bfloat16),

time: 155 us -> 154 us (level)
    all_to_all x1, waiting for transfers between devices: 2.31 us -> 0.01 us  [across(): lax.all_to_all(value, 'grid', split_axis=0, concat_axis=0, tiled=True)]
  transfers between devices with their start and end apart: 30 -> 30, of which waited for: 20 -> 19; matrix products, arithmetic and copies ran while one was open for 1% -> 1% of each run, Pallas kernels for 10% -> 12%
where the time goes in v2:
time: 154 us
  waiting for transfers between devices  67.3 us (44%)
  starting transfers between devices  42.6 us (28%)
  Pallas kernels  36.5 us (24%)
  local copies, waits for them, and re-layouts  4.71 us (3%)
  between operations  1.57 us (1%)
    ppermute x29, waiting for transfers between devices, swap(): return lax.ppermute(value, axis, [(i, i ^ offset) for i in range(size)])  67.3 us
    ppermute x29, starting transfers between devices, swap(): return lax.ppermute(value, axis, [(i, i ^ offset) for i in range(size)])  35.9 us
    pallas_call x2, Pallas kernels, forward(): pl.pallas_call(functools.partial(forward_kernel, plan, piece, 1.0 / all_b...  12.7 us
    pallas_call x1, Pallas kernels, body(): pl.pallas_call(functools.partial(backward_kernel, n, count, tiles_dev, pi...  10.8 us
    all_to_all x1, starting transfers between devices, across(): lax.all_to_all(value, 'grid', split_axis=0, concat_axis=0, tiled=True)  6.69 us
    pallas_call x2, Pallas kernels, body(): pl.pallas_call(functools.partial(unpack_kernel, groups, per, tuple(offset...  5.5 us
    pallas_call x1, Pallas kernels, body(): pl.pallas_call(functools.partial(pack_kernel, groups, per), out_shape=[ja...  3.56 us
  transfers between devices with their start and end apart: 30, of which 19 were waited for; matrix products, arithmetic and copies ran while one was open for 1% of the time, Pallas kernels for 12%

profile of v2, /device:TPU:8, one launch (start us, length us, event | category | flops | bytes accessed | tf_op | source)
XLA Modules:
  0.0 153.7 jit_solution(11426390695784792359)
XLA Ops:
  8.0 3.6 %pack.1 = (bf16[8,208,512]{2,1,0:T(8,128)(2,1)}, bf16[8,48,512]{2,1,0:T(8,128)(2,1)}) custom-call(s32[16]{0:T(128)} %rows_ref.5, bf16[16,16,3840]{2,1,0:T(8,128)(2,1)} %coef_ref.1), custom_call_target="tpu_custom_call" | custom-call | tf_op jit(solution)/shard_map/pack/pallas_call | solution.py:350
  11.6 7.4 %collective-permute-done.2 = bf16[144,640]{1,0:T(8,128)(2,1)S(1)} collective-permute-done((bf16[144,640]{1,0:T(8,128)(2,1)S(1)}, bf16[144,640]{1,0:T(8,128)(2,1)S(1)}, u32[]{:S(2)}, u32[]{:S(2)}) %collective-permute-start.2) | collective-permute-done | bytes 184352 | tf_op jit(solution)/shard_map/ppermute | solution.py:285
  19.0 2.0 %collective-permute-done.1 = bf16[144,640]{1,0:T(8,128)(2,1)S(1)} collective-permute-done((bf16[144,640]{1,0:T(8,128)(2,1)S(1)}, bf16[144,640]{1,0:T(8,128)(2,1)S(1)}, u32[]{:S(2)}, u32[]{:S(2)}) %collective-permute-start.1) | collective-permute-done | bytes 184352 | tf_op jit(solution)/shard_map/ppermute | solution.py:285
  21.0 6.7 %all-to-all-start.2 = ((bf16[8,208,512]{2,1,0:T(8,128)(2,1)}), bf16[8,208,512]{2,1,0:T(8,128)(2,1)}, u32[]{:S(2)}, u32[]{:S(2)}) async-start(bf16[8,208,512]{2,1,0:T(8,128)(2,1)} %get-tuple-element.138), calls=%async_computation.2 | async-start | bytes 3407872 | tf_op jit(solution)/shard_map/all_to_all | solution.py:320
  34.8 13.5 %collective-permute-done.4.refs_5_.refs_4_ = bf16[1,144,640]{2,1,0:T(8,128)(2,1)S(1)} collective-permute-done((bf16[1,144,640]{2,1,0:T(8,128)(2,1)S(1)}, bf16[1,144,640]{2,1,0:T(8,128)(2,1)S(1)}, u32[]{:S(2)}, u32[]{:S(2)}) %collective-permute-start.4) | collective-permute-done | bytes 184352 | tf_op jit(solution)/shard_map/ppermute | solution.py:285
  48.2 2.0 %collective-permute-done.7.refs_2_.refs_12_ = bf16[1,144,640]{2,1,0:T(8,128)(2,1)S(1)} collective-permute-done((bf16[1,144,640]{2,1,0:T(8,128)(2,1)S(1)}, bf16[1,144,640]{2,1,0:T(8,128)(2,1)S(1)}, u32[]{:S(2)}, u32[]{:S(2)}) %collective-permute-start.7) | collective-permute-done | bytes 184352 | tf_op jit(solution)/shard_map/ppermute | solution.py:285
  50.2 7.0 %collective-permute-done.6.refs_3_.refs_10_.refs_9_ = bf16[3,144,640]{2,1,0:T(8,128)(2,1)S(1)} collective-permute-done((bf16[3,144,640]{2,1,0:T(8,128)(2,1)S(1)}, bf16[3,144,640]{2,1,0:T(8,128)(2,1)S(1)}, u32[]{:S(2)}, u32[]{:S(2)}) %collective-permute-start.6) | collective-permute-done | bytes 552992 | tf_op jit(solution)/shard_map/ppermute | solution.py:285
  64.4 8.6 %forward.6 = (f32[16,640]{1,0:T(8,128)}, bf16[128,16,512]{2,1,0:T(8,128)(2,1)}) custom-call(s32[16,16]{1,0:T(8,128)S(1)} %get-tuple-element.133.touch_ref, s32[8,16]{1,0:T(8,128)S(1)} %get-tuple-element.134.rows_ref, s32[2]{0:T(128)S(1)} %pad_add_fusion.at_ref, f32[512,128]{1,0:T(8,128)S(1)} %get-tuple-element.137.weight_ref, ...), custom_call_target="tpu_custom_call" | custom-call | flops 2013265920 | bytes 134217728 | tf_op jit(solution)/shard_map/forward/pallas_call | solution.py:434
  77.2 4.1 %forward.7 = f32[16,640]{1,0:T(8,128)S(1)} custom-call(s32[16,16]{1,0:T(8,128)S(1)} %get-tuple-element.133.touch_ref, s32[8,16]{1,0:T(8,128)S(1)} %get-tuple-element.134.rows_ref, s32[2]{0:T(128)S(1)} %pad_add_fusion.at_ref, f32[512,128]{1,0:T(8,128)S(1)} %get-tuple-element.137.weight_ref, f32[16,640]{1,0:T(8,128)} %get-tuple-element.143.refs_0_, ...), custom_call_target="tpu_custom_call" | custom-call | flops 671088640 | bytes 134217728 | tf_op jit(solution)/shard_map/forward/pallas_call | solution.py:434
  84.3 2.5 %collective-permute-done.18 = f32[16,640]{1,0:T(8,128)S(1)} collective-permute-done((f32[16,640]{1,0:T(8,128)S(1)}, f32[16,640]{1,0:T(8,128)S(1)}, u32[]{:S(2)}, u32[]{:S(2)}) %collective-permute-start.18) | collective-permute-done | bytes 40992 | tf_op jit(solution)/shard_map/ppermute | solution.py:285
  86.8 2.5 %collective-permute-start.19 = (f32[16,640]{1,0:T(8,128)S(1)}, f32[16,640]{1,0:T(8,128)S(1)}, u32[]{:S(2)}, u32[]{:S(2)}) collective-permute-start(f32[16,640]{1,0:T(8,128)S(1)} %add.19), channel_id=1, source_target_pairs={{0,1},{1,0},{2,3},{3,2},{4,5},{5,4},{6,7},{7,6},{8,9},{9,8},{10,11... | collective-permute-start | bytes 122888 | tf_op jit(solution)/shard_map/ppermute | solution.py:285
  89.3 2.0 %collective-permute-done.19 = f32[16,640]{1,0:T(8,128)S(1)} collective-permute-done((f32[16,640]{1,0:T(8,128)S(1)}, f32[16,640]{1,0:T(8,128)S(1)}, u32[]{:S(2)}, u32[]{:S(2)}) %collective-permute-start.19) | collective-permute-done | bytes 40992 | tf_op jit(solution)/shard_map/ppermute | solution.py:285
  91.3 2.0 %collective-permute-start.20 = (f32[16,640]{1,0:T(8,128)S(1)}, f32[16,640]{1,0:T(8,128)S(1)}, u32[]{:S(2)}, u32[]{:S(2)}) collective-permute-start(f32[16,640]{1,0:T(8,128)S(1)} %add.20), channel_id=1, source_target_pairs={{0,2},{1,3},{2,0},{3,1},{4,6},{5,7},{6,4},{7,5},{8,10},{9,11},{10,... | collective-permute-start | bytes 122888 | tf_op jit(solution)/shard_map/ppermute | solution.py:285
  93.3 2.0 %collective-permute-done.20 = f32[16,640]{1,0:T(8,128)S(1)} collective-permute-done((f32[16,640]{1,0:T(8,128)S(1)}, f32[16,640]{1,0:T(8,128)S(1)}, u32[]{:S(2)}, u32[]{:S(2)}) %collective-permute-start.20) | collective-permute-done | bytes 40992 | tf_op jit(solution)/shard_map/ppermute | solution.py:285
  95.3 3.9 %collective-permute-start.21 = (f32[16,640]{1,0:T(8,128)S(1)}, f32[16,640]{1,0:T(8,128)S(1)}, u32[]{:S(2)}, u32[]{:S(2)}) collective-permute-start(f32[16,640]{1,0:T(8,128)S(1)} %add.21), channel_id=1, source_target_pairs={{0,4},{1,5},{2,6},{3,7},{4,0},{5,1},{6,2},{7,3},{8,12},{9,13},{10,... | collective-permute-start | bytes 122888 | tf_op jit(solution)/shard_map/ppermute | solution.py:285
  99.1 2.0 %collective-permute-done.21 = f32[16,640]{1,0:T(8,128)S(1)} collective-permute-done((f32[16,640]{1,0:T(8,128)S(1)}, f32[16,640]{1,0:T(8,128)S(1)}, u32[]{:S(2)}, u32[]{:S(2)}) %collective-permute-start.21) | collective-permute-done | bytes 40992 | tf_op jit(solution)/shard_map/ppermute | solution.py:285
  101.8 10.8 %backward.1 = (bf16[208,512]{1,0:T(8,128)(2,1)}, bf16[208,512]{1,0:T(8,128)(2,1)}, bf16[208,512]{1,0:T(8,128)(2,1)}, bf16[208,512]{1,0:T(8,128)(2,1)}, bf16[208,...) custom-call(s32[16,16]{1,0:T(8,128)S(1)} %get-tuple-element.133.touc, ...), custom_call_target="tpu_custom_call" | custom-call | tf_op jit(solution)/shard_map/backward/pallas_call | solution.py:474
  113.9 2.9 %collective-permute-start.26 = (bf16[208,512]{1,0:T(8,128)(2,1)}, bf16[208,512]{1,0:T(8,128)(2,1)S(1)}, u32[]{:S(2)}, u32[]{:S(2)}) collective-permute-start(bf16[208,512]{1,0:T(8,128)(2,1)} %get-tuple-element.156), channel_id=1, source_target_pairs={{0,4},{1,5},{2,6},{3,7},{4,0},{5,1},{6,2},{7,3},{8,12},{9,13},{10,... | collective-permute-start | bytes 638984 | tf_op jit(solution)/shard_map/ppermute | solution.py:285
  120.5 3.1 %collective-permute-start.22 = (bf16[208,512]{1,0:T(8,128)(2,1)}, bf16[208,512]{1,0:T(8,128)(2,1)S(1)}, u32[]{:S(2)}, u32[]{:S(2)}) collective-permute-start(bf16[208,512]{1,0:T(8,128)(2,1)} %get-tuple-element.151), channel_id=1, source_target_pairs={{0,6},{1,7},{2,4},{3,5},{4,2},{5,3},{6,0},{7,1},{8,14},{9,15},{10,... | collective-permute-start | bytes 638984 | tf_op jit(solution)/shard_map/ppermute | solution.py:285
  126.9 4.6 %collective-permute-done.26.refs_3_ = bf16[208,512]{1,0:T(8,128)(2,1)S(1)} collective-permute-done((bf16[208,512]{1,0:T(8,128)(2,1)}, bf16[208,512]{1,0:T(8,128)(2,1)S(1)}, u32[]{:S(2)}, u32[]{:S(2)}) %collective-permute-start.26) | collective-permute-done | bytes 213024 | tf_op jit(solution)/shard_map/ppermute | solution.py:285
  131.5 10.1 %collective-permute-done.27.refs_4_ = bf16[208,512]{1,0:T(8,128)(2,1)S(1)} collective-permute-done((bf16[208,512]{1,0:T(8,128)(2,1)}, bf16[208,512]{1,0:T(8,128)(2,1)S(1)}, u32[]{:S(2)}, u32[]{:S(2)}) %collective-permute-start.27) | collective-permute-done | bytes 213024 | tf_op jit(solution)/shard_map/ppermute | solution.py:285
  142.4 3.2 %unpack.2.refs_2_ = f32[16,16,3840]{2,1,0:T(8,128)} custom-call(s32[16]{0:T(128)} %rows_ref.5, s32[2]{0:T(128)S(1)} %pad_add_fusion.at_ref, bf16[8,48,512]{2,1,0:T(8,128)(2,1)S(1)} %get-tuple-element.166.spill_ref, bf16[208,512]{1,0:T(8,128)(2,1)} %get-tuple-element.153.refs_0_, bf16[208,512]{1,0:T(8,128)(2,1)} %copy-done.1, bf16[208,512]{1,0:T(8,128)(2,1)} %copy-done.2, ...), custom_call_target="tpu_custom_call" | custom-call | bytes 4194304 | tf_op jit(solution)/shard_map/unpack/pallas_call | solution.py:491
  147.3 3.3 %collective-permute-done.23.refs_1_ = bf16[208,512]{1,0:T(8,128)(2,1)S(1)} collective-permute-done((bf16[208,512]{1,0:T(8,128)(2,1)}, bf16[208,512]{1,0:T(8,128)(2,1)S(1)}, u32[]{:S(2)}, u32[]{:S(2)}) %collective-permute-start.23) | collective-permute-done | bytes 213024 | tf_op jit(solution)/shard_map/ppermute | solution.py:285
  151.2 2.3 %unpack.3 = f32[16,16,3840]{2,1,0:T(8,128)} custom-call(s32[16]{0:T(128)} %rows_ref.5, s32[2]{0:T(128)S(1)} %pad_add_fusion.at_ref, bf16[8,48,512]{2,1,0:T(8,128)(2,1)S(1)} %get-tuple-element.166.spill_ref, bf16[208,512]{1,0:T(8,128)(2,1)} %copy-done.5, bf16[208,512]{1,0:T(8,128)(2,1)} %copy-done.7, ...), custom_call_target="tpu_custom_call", output_to_operand_aliasing={{}: (5, {})} | custom-call | bytes 4194304 | tf_op jit(solution)/shard_map/unpack/pallas_call | solution.py:491
  (80 shorter events, 40.0 us)
Async XLA Ops:
  2.4 9.2 %collective-permute-start.3 = (bf16[1,144,640]{2,1,0:T(8,128)(2,1)S(1)}, bf16[1,144,640]{2,1,0:T(8,128)(2,1)S(1)}, u32[]{:S(2)}, u32[]{:S(2)}) collective-permute-start(bf16[1,144,640]{2,1,0:T(8,128)(2,1)S(1)} %bitcast.9), channel_id=1, source_target_pairs={{0,1},{1,0},{2,3},{3,2},{4,5},{5,4},{6,7},{7,6},{8,9},{9,8},{10,11... | collective-permute-start | bytes 552968 | tf_op jit(solution)/shard_map/ppermute | solution.py:285
  4.0 15.0 %collective-permute-start.2 = (bf16[144,640]{1,0:T(8,128)(2,1)S(1)}, bf16[144,640]{1,0:T(8,128)(2,1)S(1)}, u32[]{:S(2)}, u32[]{:S(2)}) collective-permute-start(bf16[144,640]{1,0:T(8,128)(2,1)S(1)} %prep.1), channel_id=1, source_target_pairs={{0,6},{1,7},{2,4},{3,5},{4,2},{5,3},{6,0},{7,1},{8,14},{9,15},{10,... | collective-permute-start | bytes 552968 | tf_op jit(solution)/shard_map/ppermute | solution.py:285
  5.5 15.5 %collective-permute-start.1 = (bf16[144,640]{1,0:T(8,128)(2,1)S(1)}, bf16[144,640]{1,0:T(8,128)(2,1)S(1)}, u32[]{:S(2)}, u32[]{:S(2)}) collective-permute-start(bf16[144,640]{1,0:T(8,128)(2,1)S(1)} %prep.1), channel_id=1, source_target_pairs={{0,4},{1,5},{2,6},{3,7},{4,0},{5,1},{6,2},{7,3},{8,12},{9,13},{10,... | collective-permute-start | bytes 552968 | tf_op jit(solution)/shard_map/ppermute | solution.py:285
  6.8 14.2 %collective-permute-start = (bf16[144,640]{1,0:T(8,128)(2,1)S(1)}, bf16[144,640]{1,0:T(8,128)(2,1)S(1)}, u32[]{:S(2)}, u32[]{:S(2)}) collective-permute-start(bf16[144,640]{1,0:T(8,128)(2,1)S(1)} %prep.1), channel_id=1, source_target_pairs={{0,2},{1,3},{2,0},{3,1},{4,6},{5,7},{6,4},{7,5},{8,10},{9,11},{10,... | collective-permute-start | bytes 552968 | tf_op jit(solution)/shard_map/ppermute | solution.py:285
  21.0 43.4 %all-to-all-start.2 = ((bf16[8,208,512]{2,1,0:T(8,128)(2,1)}), bf16[8,208,512]{2,1,0:T(8,128)(2,1)}, u32[]{:S(2)}, u32[]{:S(2)}) async-start(bf16[8,208,512]{2,1,0:T(8,128)(2,1)} %get-tuple-element.138), calls=%async_computation.2 | async-start | bytes 3407872 | tf_op jit(solution)/shard_map/all_to_all | solution.py:320
  27.8 29.5 %collective-permute-start.6 = (bf16[3,144,640]{2,1,0:T(8,128)(2,1)S(1)}, bf16[3,144,640]{2,1,0:T(8,128)(2,1)S(1)}, u32[]{:S(2)}, u32[]{:S(2)}) collective-permute-start(bf16[3,144,640]{2,1,0:T(8,128)(2,1)S(1)} %pad_maximum_fusion.after_ref.refs_1_.refs_2_), channel_id=1, source_target_pairs={{0,1},{1,0},{2,3},{3,2},{4,5},{5,4},{6,7},{7,6},{8,9},{9,8},{10,11... | collective-permute-start | bytes 1658888 | tf_op jit(solution)/shard_map/ppermute | solution.py:285
  29.3 27.9 %collective-permute-start.5 = (bf16[3,144,640]{2,1,0:T(8,128)(2,1)S(1)}, bf16[3,144,640]{2,1,0:T(8,128)(2,1)S(1)}, u32[]{:S(2)}, u32[]{:S(2)}) collective-permute-start(bf16[3,144,640]{2,1,0:T(8,128)(2,1)S(1)} %pad_maximum_fusion.after_ref.refs_1_.refs_2_), channel_id=1, source_target_pairs={{0,16},{8,24},{16,0},{24,8},{1,17},{9,25},{17,1},{25,9},{2,18},{10... | collective-permute-start | bytes 1658888 | tf_op jit(solution)/shard_map/ppermute | solution.py:285
  30.8 17.4 %collective-permute-start.4 = (bf16[1,144,640]{2,1,0:T(8,128)(2,1)S(1)}, bf16[1,144,640]{2,1,0:T(8,128)(2,1)S(1)}, u32[]{:S(2)}, u32[]{:S(2)}) collective-permute-start(bf16[1,144,640]{2,1,0:T(8,128)(2,1)S(1)} %bitcast.10), channel_id=1, source_target_pairs={{0,16},{8,24},{16,0},{24,8},{1,17},{9,25},{17,1},{25,9},{2,18},{10... | collective-permute-start | bytes 552968 | tf_op jit(solution)/shard_map/ppermute | solution.py:285
  31.3 18.9 %collective-permute-start.7 = (bf16[1,144,640]{2,1,0:T(8,128)(2,1)S(1)}, bf16[1,144,640]{2,1,0:T(8,128)(2,1)S(1)}, u32[]{:S(2)}, u32[]{:S(2)}) collective-permute-start(bf16[1,144,640]{2,1,0:T(8,128)(2,1)S(1)} %collective-permute-done.3.refs_2_.refs_9_.refs_8_), channel_id=1, source_target_pairs={{0,16},{8,24},{16,0},{24,8},{1,17},{9,25},{17,1},{25,9},{2,18},{10... | collective-permute-start | bytes 552968 | tf_op jit(solution)/shard_map/ppermute | solution.py:285
  57.3 6.5 %collective-permute-start.12 = (bf16[3,144,640]{2,1,0:T(8,128)(2,1)S(1)}, bf16[3,144,640]{2,1,0:T(8,128)(2,1)}, u32[]{:S(2)}, u32[]{:S(2)}) collective-permute-start(bf16[3,144,640]{2,1,0:T(8,128)(2,1)S(1)} %collective-permute-done.5.refs_6_.refs_5_), channel_id=1, source_target_pairs={{0,8},{8,0},{16,24},{24,16},{1,9},{9,1},{17,25},{25,17},{2,10},{10... | collective-permute-start | bytes 1658888 | tf_op jit(solution)/shard_map/ppermute | solution.py:285
  57.3 6.5 %collective-permute-start.10 = (bf16[3,144,640]{2,1,0:T(8,128)(2,1)S(1)}, bf16[3,144,640]{2,1,0:T(8,128)(2,1)}, u32[]{:S(2)}, u32[]{:S(2)}) collective-permute-start(bf16[3,144,640]{2,1,0:T(8,128)(2,1)S(1)} %pad_maximum_fusion.after_ref.refs_1_.refs_2_), channel_id=1, source_target_pairs={{0,8},{8,0},{16,24},{24,16},{1,9},{9,1},{17,25},{25,17},{2,10},{10... | collective-permute-start | bytes 1658888 | tf_op jit(solution)/shard_map/ppermute | solution.py:285
  57.8 6.7 %collective-permute-start.14 = (bf16[3,144,640]{2,1,0:T(8,128)(2,1)S(1)}, bf16[3,144,640]{2,1,0:T(8,128)(2,1)}, u32[]{:S(2)}, u32[]{:S(2)}) collective-permute-start(bf16[3,144,640]{2,1,0:T(8,128)(2,1)S(1)} %collective-permute-done.6.refs_3_.refs_10_.refs_9_), channel_id=1, source_target_pairs={{0,8},{8,0},{16,24},{24,16},{1,9},{9,1},{17,25},{25,17},{2,10},{10... | collective-permute-start | bytes 1658888 | tf_op jit(solution)/shard_map/ppermute | solution.py:285
  60.2 14.8 %collective-permute-start.8 = (bf16[3,144,640]{2,1,0:T(8,128)(2,1)S(1)}, bf16[3,144,640]{2,1,0:T(8,128)(2,1)S(1)}, u32[]{:S(2)}, u32[]{:S(2)}) collective-permute-start(bf16[3,144,640]{2,1,0:T(8,128)(2,1)S(1)} %collective-permute-done.6.refs_3_.refs_10_.refs_9_), channel_id=1, source_target_pairs={{0,16},{8,24},{16,0},{24,8},{1,17},{9,25},{17,1},{25,9},{2,18},{10... | collective-permute-start | bytes 1658888 | tf_op jit(solution)/shard_map/ppermute | solution.py:285
  82.8 4.0 %collective-permute-start.18 = (f32[16,640]{1,0:T(8,128)S(1)}, f32[16,640]{1,0:T(8,128)S(1)}, u32[]{:S(2)}, u32[]{:S(2)}) collective-permute-start(f32[16,640]{1,0:T(8,128)S(1)} %add.18), channel_id=1, source_target_pairs={{0,16},{8,24},{16,0},{24,8},{1,17},{9,25},{17,1},{25,9},{2,18},{10... | collective-permute-start | bytes 122888 | tf_op jit(solution)/shard_map/ppermute | solution.py:285
  86.8 4.5 %collective-permute-start.19 = (f32[16,640]{1,0:T(8,128)S(1)}, f32[16,640]{1,0:T(8,128)S(1)}, u32[]{:S(2)}, u32[]{:S(2)}) collective-permute-start(f32[16,640]{1,0:T(8,128)S(1)} %add.19), channel_id=1, source_target_pairs={{0,1},{1,0},{2,3},{3,2},{4,5},{5,4},{6,7},{7,6},{8,9},{9,8},{10,11... | collective-permute-start | bytes 122888 | tf_op jit(solution)/shard_map/ppermute | solution.py:285
  91.3 4.0 %collective-permute-start.20 = (f32[16,640]{1,0:T(8,128)S(1)}, f32[16,640]{1,0:T(8,128)S(1)}, u32[]{:S(2)}, u32[]{:S(2)}) collective-permute-start(f32[16,640]{1,0:T(8,128)S(1)} %add.20), channel_id=1, source_target_pairs={{0,2},{1,3},{2,0},{3,1},{4,6},{5,7},{6,4},{7,5},{8,10},{9,11},{10,... | collective-permute-start | bytes 122888 | tf_op jit(solution)/shard_map/ppermute | solution.py:285
  95.3 5.9 %collective-permute-start.21 = (f32[16,640]{1,0:T(8,128)S(1)}, f32[16,640]{1,0:T(8,128)S(1)}, u32[]{:S(2)}, u32[]{:S(2)}) collective-permute-start(f32[16,640]{1,0:T(8,128)S(1)} %add.21), channel_id=1, source_target_pairs={{0,4},{1,5},{2,6},{3,7},{4,0},{5,1},{6,2},{7,3},{8,12},{9,13},{10,... | collective-permute-start | bytes 122888 | tf_op jit(solution)/shard_map/ppermute | solution.py:285
  112.6 7.9 %collective-permute-start.24 = (bf16[208,512]{1,0:T(8,128)(2,1)}, bf16[208,512]{1,0:T(8,128)(2,1)S(1)}, u32[]{:S(2)}, u32[]{:S(2)}) collective-permute-start(bf16[208,512]{1,0:T(8,128)(2,1)} %get-tuple-element.154), channel_id=1, source_target_pairs={{0,1},{1,0},{2,3},{3,2},{4,5},{5,4},{6,7},{7,6},{8,9},{9,8},{10,11... | collective-permute-start | bytes 638984 | tf_op jit(solution)/shard_map/ppermute | solution.py:285
  113.7 9.9 %collective-permute-start.25 = (bf16[208,512]{1,0:T(8,128)(2,1)}, bf16[208,512]{1,0:T(8,128)(2,1)S(1)}, u32[]{:S(2)}, u32[]{:S(2)}) collective-permute-start(bf16[208,512]{1,0:T(8,128)(2,1)} %get-tuple-element.155), channel_id=1, source_target_pairs={{0,2},{1,3},{2,0},{3,1},{4,6},{5,7},{6,4},{7,5},{8,10},{9,11},{10,... | collective-permute-start | bytes 638984 | tf_op jit(solution)/shard_map/ppermute | solution.py:285
  113.9 17.6 %collective-permute-start.26 = (bf16[208,512]{1,0:T(8,128)(2,1)}, bf16[208,512]{1,0:T(8,128)(2,1)S(1)}, u32[]{:S(2)}, u32[]{:S(2)}) collective-permute-start(bf16[208,512]{1,0:T(8,128)(2,1)} %get-tuple-element.156), channel_id=1, source_target_pairs={{0,4},{1,5},{2,6},{3,7},{4,0},{5,1},{6,2},{7,3},{8,12},{9,13},{10,... | collective-permute-start | bytes 638984 | tf_op jit(solution)/shard_map/ppermute | solution.py:285
  116.8 24.8 %collective-permute-start.27 = (bf16[208,512]{1,0:T(8,128)(2,1)}, bf16[208,512]{1,0:T(8,128)(2,1)S(1)}, u32[]{:S(2)}, u32[]{:S(2)}) collective-permute-start(bf16[208,512]{1,0:T(8,128)(2,1)} %get-tuple-element.157), channel_id=1, source_target_pairs={{0,5},{1,4},{2,7},{3,6},{4,1},{5,0},{6,3},{7,2},{8,13},{9,12},{10,... | collective-permute-start | bytes 638984 | tf_op jit(solution)/shard_map/ppermute | solution.py:285
  118.1 23.5 %collective-permute-start.28 = (bf16[208,512]{1,0:T(8,128)(2,1)}, bf16[208,512]{1,0:T(8,128)(2,1)S(1)}, u32[]{:S(2)}, u32[]{:S(2)}) collective-permute-start(bf16[208,512]{1,0:T(8,128)(2,1)} %get-tuple-element.158), channel_id=1, source_target_pairs={{0,3},{1,2},{2,1},{3,0},{4,7},{5,6},{6,5},{7,4},{8,11},{9,10},{10,... | collective-permute-start | bytes 638984 | tf_op jit(solution)/shard_map/ppermute | solution.py:285
  120.5 26.8 %collective-permute-start.22 = (bf16[208,512]{1,0:T(8,128)(2,1)}, bf16[208,512]{1,0:T(8,128)(2,1)S(1)}, u32[]{:S(2)}, u32[]{:S(2)}) collective-permute-start(bf16[208,512]{1,0:T(8,128)(2,1)} %get-tuple-element.151), channel_id=1, source_target_pairs={{0,6},{1,7},{2,4},{3,5},{4,2},{5,3},{6,0},{7,1},{8,14},{9,15},{10,... | collective-permute-start | bytes 638984 | tf_op jit(solution)/shard_map/ppermute | solution.py:285
  123.6 27.0 %collective-permute-start.23 = (bf16[208,512]{1,0:T(8,128)(2,1)}, bf16[208,512]{1,0:T(8,128)(2,1)S(1)}, u32[]{:S(2)}, u32[]{:S(2)}) collective-permute-start(bf16[208,512]{1,0:T(8,128)(2,1)} %get-tuple-element.152), channel_id=1, source_target_pairs={{0,7},{1,6},{2,5},{3,4},{4,3},{5,2},{6,1},{7,0},{8,15},{9,14},{10,... | collective-permute-start | bytes 638984 | tf_op jit(solution)/shard_map/ppermute | solution.py:285
  (18 other events, 111.5 us)

commit v3 on v2

--- a/solution.py
+++ b/solution.py
@@ -498,7 +498,7 @@
                 pltpu.SemaphoreType.DMA((len(offsets),)),
             ],
             input_output_aliases={3 + len(offsets): 0} if before else {},
-            compiler_params=params,
+            compiler_params=pltpu.CompilerParams(vmem_limit_bytes=big_vmem // 4),
             cost_estimate=pl.CostEstimate(flops=0, bytes_accessed=1 << 22, transcendentals=0),
             name="unpack",
         )(block_rows, at, spill, *[returned[d] for d in offsets], *before)

time: 154 us -> 153 us (level)
  transfers between devices with their start and end apart: 30 -> 30, of which waited for: 19 -> 19; matrix products, arithmetic and copies ran while one was open for 1% -> 1% of each run, Pallas kernels for 12% -> 11%
where the time goes in v3:
time: 153 us
  waiting for transfers between devices  68 us (44%)
  starting transfers between devices  42.6 us (28%)
  Pallas kernels  35.2 us (23%)
  local copies, waits for them, and re-layouts  4.24 us (3%)
    ppermute x29, waiting for transfers between devices, swap(): return lax.ppermute(value, axis, [(i, i ^ offset) for i in range(size)])  68 us
    ppermute x29, starting transfers between devices, swap(): return lax.ppermute(value, axis, [(i, i ^ offset) for i in range(size)])  35.9 us
    pallas_call x2, Pallas kernels, forward(): pl.pallas_call(functools.partial(forward_kernel, plan, piece, 1.0 / all_b...  12.7 us
    pallas_call x1, Pallas kernels, body(): pl.pallas_call(functools.partial(backward_kernel, n, count, tiles_dev, pi...  10.8 us
    all_to_all x1, starting transfers between devices, across(): lax.all_to_all(value, 'grid', split_axis=0, concat_axis=0, tiled=True)  6.7 us
    pallas_call x2, Pallas kernels, body(): pl.pallas_call(functools.partial(unpack_kernel, groups, per, tuple(offset...  4.16 us
    pallas_call x1, Pallas kernels, body(): pl.pallas_call(functools.partial(pack_kernel, groups, per), out_shape=[ja...  3.55 us
  transfers between devices with their start and end apart: 30, of which 19 were waited for; matrix products, arithmetic and copies ran while one was open for 1% of the time, Pallas kernels for 11%

profile of v3, /device:TPU:8, one launch (start us, length us, event | category | flops | bytes accessed | tf_op | source)
XLA Modules:
  0.0 152.5 jit_solution(11281846370825327394)
XLA Ops:
  8.0 3.5 %pack.1 = (bf16[8,208,512]{2,1,0:T(8,128)(2,1)}, bf16[8,48,512]{2,1,0:T(8,128)(2,1)}) custom-call(s32[16]{0:T(128)} %rows_ref.5, bf16[16,16,3840]{2,1,0:T(8,128)(2,1)} %coef_ref.1), custom_call_target="tpu_custom_call" | custom-call | tf_op jit(solution)/shard_map/pack/pallas_call | solution.py:350
  11.6 7.4 %collective-permute-done.2 = bf16[144,640]{1,0:T(8,128)(2,1)S(1)} collective-permute-done((bf16[144,640]{1,0:T(8,128)(2,1)S(1)}, bf16[144,640]{1,0:T(8,128)(2,1)S(1)}, u32[]{:S(2)}, u32[]{:S(2)}) %collective-permute-start.2) | collective-permute-done | bytes 184352 | tf_op jit(solution)/shard_map/ppermute | solution.py:285
  19.0 2.0 %collective-permute-done.1 = bf16[144,640]{1,0:T(8,128)(2,1)S(1)} collective-permute-done((bf16[144,640]{1,0:T(8,128)(2,1)S(1)}, bf16[144,640]{1,0:T(8,128)(2,1)S(1)}, u32[]{:S(2)}, u32[]{:S(2)}) %collective-permute-start.1) | collective-permute-done | bytes 184352 | tf_op jit(solution)/shard_map/ppermute | solution.py:285
  21.0 6.7 %all-to-all-start.2 = ((bf16[8,208,512]{2,1,0:T(8,128)(2,1)}), bf16[8,208,512]{2,1,0:T(8,128)(2,1)}, u32[]{:S(2)}, u32[]{:S(2)}) async-start(bf16[8,208,512]{2,1,0:T(8,128)(2,1)} %get-tuple-element.138), calls=%async_computation.2 | async-start | bytes 3407872 | tf_op jit(solution)/shard_map/all_to_all | solution.py:320
  34.8 13.5 %collective-permute-done.4.refs_5_.refs_4_ = bf16[1,144,640]{2,1,0:T(8,128)(2,1)S(1)} collective-permute-done((bf16[1,144,640]{2,1,0:T(8,128)(2,1)S(1)}, bf16[1,144,640]{2,1,0:T(8,128)(2,1)S(1)}, u32[]{:S(2)}, u32[]{:S(2)}) %collective-permute-start.4) | collective-permute-done | bytes 184352 | tf_op jit(solution)/shard_map/ppermute | solution.py:285
  48.2 2.0 %collective-permute-done.7.refs_2_.refs_12_ = bf16[1,144,640]{2,1,0:T(8,128)(2,1)S(1)} collective-permute-done((bf16[1,144,640]{2,1,0:T(8,128)(2,1)S(1)}, bf16[1,144,640]{2,1,0:T(8,128)(2,1)S(1)}, u32[]{:S(2)}, u32[]{:S(2)}) %collective-permute-start.7) | collective-permute-done | bytes 184352 | tf_op jit(solution)/shard_map/ppermute | solution.py:285
  50.2 7.0 %collective-permute-done.6.refs_3_.refs_10_.refs_9_ = bf16[3,144,640]{2,1,0:T(8,128)(2,1)S(1)} collective-permute-done((bf16[3,144,640]{2,1,0:T(8,128)(2,1)S(1)}, bf16[3,144,640]{2,1,0:T(8,128)(2,1)S(1)}, u32[]{:S(2)}, u32[]{:S(2)}) %collective-permute-start.6) | collective-permute-done | bytes 552992 | tf_op jit(solution)/shard_map/ppermute | solution.py:285
  64.5 8.6 %forward.6 = (f32[16,640]{1,0:T(8,128)}, bf16[128,16,512]{2,1,0:T(8,128)(2,1)}) custom-call(s32[16,16]{1,0:T(8,128)S(1)} %get-tuple-element.133.touch_ref, s32[8,16]{1,0:T(8,128)S(1)} %get-tuple-element.134.rows_ref, s32[2]{0:T(128)S(1)} %pad_add_fusion.at_ref, f32[512,128]{1,0:T(8,128)S(1)} %get-tuple-element.137.weight_ref, ...), custom_call_target="tpu_custom_call" | custom-call | flops 2013265920 | bytes 134217728 | tf_op jit(solution)/shard_map/forward/pallas_call | solution.py:434
  77.2 4.1 %forward.7 = f32[16,640]{1,0:T(8,128)S(1)} custom-call(s32[16,16]{1,0:T(8,128)S(1)} %get-tuple-element.133.touch_ref, s32[8,16]{1,0:T(8,128)S(1)} %get-tuple-element.134.rows_ref, s32[2]{0:T(128)S(1)} %pad_add_fusion.at_ref, f32[512,128]{1,0:T(8,128)S(1)} %get-tuple-element.137.weight_ref, f32[16,640]{1,0:T(8,128)} %get-tuple-element.143.refs_0_, ...), custom_call_target="tpu_custom_call" | custom-call | flops 671088640 | bytes 134217728 | tf_op jit(solution)/shard_map/forward/pallas_call | solution.py:434
  84.3 2.5 %collective-permute-done.18 = f32[16,640]{1,0:T(8,128)S(1)} collective-permute-done((f32[16,640]{1,0:T(8,128)S(1)}, f32[16,640]{1,0:T(8,128)S(1)}, u32[]{:S(2)}, u32[]{:S(2)}) %collective-permute-start.18) | collective-permute-done | bytes 40992 | tf_op jit(solution)/shard_map/ppermute | solution.py:285
  86.8 2.5 %collective-permute-start.19 = (f32[16,640]{1,0:T(8,128)S(1)}, f32[16,640]{1,0:T(8,128)S(1)}, u32[]{:S(2)}, u32[]{:S(2)}) collective-permute-start(f32[16,640]{1,0:T(8,128)S(1)} %add.19), channel_id=1, source_target_pairs={{0,1},{1,0},{2,3},{3,2},{4,5},{5,4},{6,7},{7,6},{8,9},{9,8},{10,11... | collective-permute-start | bytes 122888 | tf_op jit(solution)/shard_map/ppermute | solution.py:285
  89.3 2.0 %collective-permute-done.19 = f32[16,640]{1,0:T(8,128)S(1)} collective-permute-done((f32[16,640]{1,0:T(8,128)S(1)}, f32[16,640]{1,0:T(8,128)S(1)}, u32[]{:S(2)}, u32[]{:S(2)}) %collective-permute-start.19) | collective-permute-done | bytes 40992 | tf_op jit(solution)/shard_map/ppermute | solution.py:285
  91.3 2.0 %collective-permute-start.20 = (f32[16,640]{1,0:T(8,128)S(1)}, f32[16,640]{1,0:T(8,128)S(1)}, u32[]{:S(2)}, u32[]{:S(2)}) collective-permute-start(f32[16,640]{1,0:T(8,128)S(1)} %add.20), channel_id=1, source_target_pairs={{0,2},{1,3},{2,0},{3,1},{4,6},{5,7},{6,4},{7,5},{8,10},{9,11},{10,... | collective-permute-start | bytes 122888 | tf_op jit(solution)/shard_map/ppermute | solution.py:285
  93.3 2.0 %collective-permute-done.20 = f32[16,640]{1,0:T(8,128)S(1)} collective-permute-done((f32[16,640]{1,0:T(8,128)S(1)}, f32[16,640]{1,0:T(8,128)S(1)}, u32[]{:S(2)}, u32[]{:S(2)}) %collective-permute-start.20) | collective-permute-done | bytes 40992 | tf_op jit(solution)/shard_map/ppermute | solution.py:285
  95.3 3.9 %collective-permute-start.21 = (f32[16,640]{1,0:T(8,128)S(1)}, f32[16,640]{1,0:T(8,128)S(1)}, u32[]{:S(2)}, u32[]{:S(2)}) collective-permute-start(f32[16,640]{1,0:T(8,128)S(1)} %add.21), channel_id=1, source_target_pairs={{0,4},{1,5},{2,6},{3,7},{4,0},{5,1},{6,2},{7,3},{8,12},{9,13},{10,... | collective-permute-start | bytes 122888 | tf_op jit(solution)/shard_map/ppermute | solution.py:285
  99.1 2.0 %collective-permute-done.21 = f32[16,640]{1,0:T(8,128)S(1)} collective-permute-done((f32[16,640]{1,0:T(8,128)S(1)}, f32[16,640]{1,0:T(8,128)S(1)}, u32[]{:S(2)}, u32[]{:S(2)}) %collective-permute-start.21) | collective-permute-done | bytes 40992 | tf_op jit(solution)/shard_map/ppermute | solution.py:285
  101.8 10.8 %backward.1 = (bf16[208,512]{1,0:T(8,128)(2,1)}, bf16[208,512]{1,0:T(8,128)(2,1)}, bf16[208,512]{1,0:T(8,128)(2,1)}, bf16[208,512]{1,0:T(8,128)(2,1)}, bf16[208,...) custom-call(s32[16,16]{1,0:T(8,128)S(1)} %get-tuple-element.133.touc, ...), custom_call_target="tpu_custom_call" | custom-call | tf_op jit(solution)/shard_map/backward/pallas_call | solution.py:474
  114.0 2.9 %collective-permute-start.26 = (bf16[208,512]{1,0:T(8,128)(2,1)}, bf16[208,512]{1,0:T(8,128)(2,1)S(1)}, u32[]{:S(2)}, u32[]{:S(2)}) collective-permute-start(bf16[208,512]{1,0:T(8,128)(2,1)} %get-tuple-element.156), channel_id=1, source_target_pairs={{0,4},{1,5},{2,6},{3,7},{4,0},{5,1},{6,2},{7,3},{8,12},{9,13},{10,... | collective-permute-start | bytes 638984 | tf_op jit(solution)/shard_map/ppermute | solution.py:285
  120.6 3.1 %collective-permute-start.22 = (bf16[208,512]{1,0:T(8,128)(2,1)}, bf16[208,512]{1,0:T(8,128)(2,1)S(1)}, u32[]{:S(2)}, u32[]{:S(2)}) collective-permute-start(bf16[208,512]{1,0:T(8,128)(2,1)} %get-tuple-element.151), channel_id=1, source_target_pairs={{0,6},{1,7},{2,4},{3,5},{4,2},{5,3},{6,0},{7,1},{8,14},{9,15},{10,... | collective-permute-start | bytes 638984 | tf_op jit(solution)/shard_map/ppermute | solution.py:285
  126.9 4.6 %collective-permute-done.26.refs_3_ = bf16[208,512]{1,0:T(8,128)(2,1)S(1)} collective-permute-done((bf16[208,512]{1,0:T(8,128)(2,1)}, bf16[208,512]{1,0:T(8,128)(2,1)S(1)}, u32[]{:S(2)}, u32[]{:S(2)}) %collective-permute-start.26) | collective-permute-done | bytes 213024 | tf_op jit(solution)/shard_map/ppermute | solution.py:285
  131.6 10.1 %collective-permute-done.27.refs_4_ = bf16[208,512]{1,0:T(8,128)(2,1)S(1)} collective-permute-done((bf16[208,512]{1,0:T(8,128)(2,1)}, bf16[208,512]{1,0:T(8,128)(2,1)S(1)}, u32[]{:S(2)}, u32[]{:S(2)}) %collective-permute-start.27) | collective-permute-done | bytes 213024 | tf_op jit(solution)/shard_map/ppermute | solution.py:285
  142.6 2.4 %unpack.2.refs_2_ = f32[16,16,3840]{2,1,0:T(8,128)} custom-call(s32[16]{0:T(128)S(1)} %copy-done.1, s32[2]{0:T(128)S(1)} %pad_add_fusion.at_ref, bf16[8,48,512]{2,1,0:T(8,128)(2,1)S(1)} %get-tuple-element.166.spill_ref, bf16[208,512]{1,0:T(8,128)(2,1)S(1)} %copy-done, bf16[208,512]{1,0:T(8,128)(2,1)S(1)} %collective-permute-done.24.refs_1_, ...), custom_call_target="tpu_custom_call" | custom-call | bytes 4194304 | tf_op jit(solution)/shard_map/unpack/pallas_call | solution.py:491
  145.0 2.3 %collective-permute-done.22.refs_0_ = bf16[208,512]{1,0:T(8,128)(2,1)S(1)} collective-permute-done((bf16[208,512]{1,0:T(8,128)(2,1)}, bf16[208,512]{1,0:T(8,128)(2,1)S(1)}, u32[]{:S(2)}, u32[]{:S(2)}) %collective-permute-start.22) | collective-permute-done | bytes 213024 | tf_op jit(solution)/shard_map/ppermute | solution.py:285
  147.4 3.3 %collective-permute-done.23.refs_1_ = bf16[208,512]{1,0:T(8,128)(2,1)S(1)} collective-permute-done((bf16[208,512]{1,0:T(8,128)(2,1)}, bf16[208,512]{1,0:T(8,128)(2,1)S(1)}, u32[]{:S(2)}, u32[]{:S(2)}) %collective-permute-start.23) | collective-permute-done | bytes 213024 | tf_op jit(solution)/shard_map/ppermute | solution.py:285
  (70 shorter events, 39.7 us)
Async XLA Ops:
  2.4 9.2 %collective-permute-start.3 = (bf16[1,144,640]{2,1,0:T(8,128)(2,1)S(1)}, bf16[1,144,640]{2,1,0:T(8,128)(2,1)S(1)}, u32[]{:S(2)}, u32[]{:S(2)}) collective-permute-start(bf16[1,144,640]{2,1,0:T(8,128)(2,1)S(1)} %bitcast.10), channel_id=1, source_target_pairs={{0,1},{1,0},{2,3},{3,2},{4,5},{5,4},{6,7},{7,6},{8,9},{9,8},{10,11... | collective-permute-start | bytes 552968 | tf_op jit(solution)/shard_map/ppermute | solution.py:285
  4.0 15.0 %collective-permute-start.2 = (bf16[144,640]{1,0:T(8,128)(2,1)S(1)}, bf16[144,640]{1,0:T(8,128)(2,1)S(1)}, u32[]{:S(2)}, u32[]{:S(2)}) collective-permute-start(bf16[144,640]{1,0:T(8,128)(2,1)S(1)} %prep.1), channel_id=1, source_target_pairs={{0,6},{1,7},{2,4},{3,5},{4,2},{5,3},{6,0},{7,1},{8,14},{9,15},{10,... | collective-permute-start | bytes 552968 | tf_op jit(solution)/shard_map/ppermute | solution.py:285
  5.5 15.5 %collective-permute-start.1 = (bf16[144,640]{1,0:T(8,128)(2,1)S(1)}, bf16[144,640]{1,0:T(8,128)(2,1)S(1)}, u32[]{:S(2)}, u32[]{:S(2)}) collective-permute-start(bf16[144,640]{1,0:T(8,128)(2,1)S(1)} %prep.1), channel_id=1, source_target_pairs={{0,4},{1,5},{2,6},{3,7},{4,0},{5,1},{6,2},{7,3},{8,12},{9,13},{10,... | collective-permute-start | bytes 552968 | tf_op jit(solution)/shard_map/ppermute | solution.py:285
  6.8 14.2 %collective-permute-start = (bf16[144,640]{1,0:T(8,128)(2,1)S(1)}, bf16[144,640]{1,0:T(8,128)(2,1)S(1)}, u32[]{:S(2)}, u32[]{:S(2)}) collective-permute-start(bf16[144,640]{1,0:T(8,128)(2,1)S(1)} %prep.1), channel_id=1, source_target_pairs={{0,2},{1,3},{2,0},{3,1},{4,6},{5,7},{6,4},{7,5},{8,10},{9,11},{10,... | collective-permute-start | bytes 552968 | tf_op jit(solution)/shard_map/ppermute | solution.py:285
  21.0 43.5 %all-to-all-start.2 = ((bf16[8,208,512]{2,1,0:T(8,128)(2,1)}), bf16[8,208,512]{2,1,0:T(8,128)(2,1)}, u32[]{:S(2)}, u32[]{:S(2)}) async-start(bf16[8,208,512]{2,1,0:T(8,128)(2,1)} %get-tuple-element.138), calls=%async_computation.2 | async-start | bytes 3407872 | tf_op jit(solution)/shard_map/all_to_all | solution.py:320
  27.8 29.5 %collective-permute-start.6 = (bf16[3,144,640]{2,1,0:T(8,128)(2,1)S(1)}, bf16[3,144,640]{2,1,0:T(8,128)(2,1)S(1)}, u32[]{:S(2)}, u32[]{:S(2)}) collective-permute-start(bf16[3,144,640]{2,1,0:T(8,128)(2,1)S(1)} %pad_maximum_fusion.after_ref.refs_1_.refs_2_), channel_id=1, source_target_pairs={{0,1},{1,0},{2,3},{3,2},{4,5},{5,4},{6,7},{7,6},{8,9},{9,8},{10,11... | collective-permute-start | bytes 1658888 | tf_op jit(solution)/shard_map/ppermute | solution.py:285
  29.3 27.9 %collective-permute-start.5 = (bf16[3,144,640]{2,1,0:T(8,128)(2,1)S(1)}, bf16[3,144,640]{2,1,0:T(8,128)(2,1)S(1)}, u32[]{:S(2)}, u32[]{:S(2)}) collective-permute-start(bf16[3,144,640]{2,1,0:T(8,128)(2,1)S(1)} %pad_maximum_fusion.after_ref.refs_1_.refs_2_), channel_id=1, source_target_pairs={{0,16},{8,24},{16,0},{24,8},{1,17},{9,25},{17,1},{25,9},{2,18},{10... | collective-permute-start | bytes 1658888 | tf_op jit(solution)/shard_map/ppermute | solution.py:285
  30.8 17.4 %collective-permute-start.4 = (bf16[1,144,640]{2,1,0:T(8,128)(2,1)S(1)}, bf16[1,144,640]{2,1,0:T(8,128)(2,1)S(1)}, u32[]{:S(2)}, u32[]{:S(2)}) collective-permute-start(bf16[1,144,640]{2,1,0:T(8,128)(2,1)S(1)} %bitcast.11), channel_id=1, source_target_pairs={{0,16},{8,24},{16,0},{24,8},{1,17},{9,25},{17,1},{25,9},{2,18},{10... | collective-permute-start | bytes 552968 | tf_op jit(solution)/shard_map/ppermute | solution.py:285
  31.3 18.9 %collective-permute-start.7 = (bf16[1,144,640]{2,1,0:T(8,128)(2,1)S(1)}, bf16[1,144,640]{2,1,0:T(8,128)(2,1)S(1)}, u32[]{:S(2)}, u32[]{:S(2)}) collective-permute-start(bf16[1,144,640]{2,1,0:T(8,128)(2,1)S(1)} %collective-permute-done.3.refs_2_.refs_9_.refs_8_), channel_id=1, source_target_pairs={{0,16},{8,24},{16,0},{24,8},{1,17},{9,25},{17,1},{25,9},{2,18},{10... | collective-permute-start | bytes 552968 | tf_op jit(solution)/shard_map/ppermute | solution.py:285
  57.3 6.5 %collective-permute-start.12 = (bf16[3,144,640]{2,1,0:T(8,128)(2,1)S(1)}, bf16[3,144,640]{2,1,0:T(8,128)(2,1)}, u32[]{:S(2)}, u32[]{:S(2)}) collective-permute-start(bf16[3,144,640]{2,1,0:T(8,128)(2,1)S(1)} %collective-permute-done.5.refs_6_.refs_5_), channel_id=1, source_target_pairs={{0,8},{8,0},{16,24},{24,16},{1,9},{9,1},{17,25},{25,17},{2,10},{10... | collective-permute-start | bytes 1658888 | tf_op jit(solution)/shard_map/ppermute | solution.py:285
  57.3 6.5 %collective-permute-start.10 = (bf16[3,144,640]{2,1,0:T(8,128)(2,1)S(1)}, bf16[3,144,640]{2,1,0:T(8,128)(2,1)}, u32[]{:S(2)}, u32[]{:S(2)}) collective-permute-start(bf16[3,144,640]{2,1,0:T(8,128)(2,1)S(1)} %pad_maximum_fusion.after_ref.refs_1_.refs_2_), channel_id=1, source_target_pairs={{0,8},{8,0},{16,24},{24,16},{1,9},{9,1},{17,25},{25,17},{2,10},{10... | collective-permute-start | bytes 1658888 | tf_op jit(solution)/shard_map/ppermute | solution.py:285
  57.8 6.7 %collective-permute-start.14 = (bf16[3,144,640]{2,1,0:T(8,128)(2,1)S(1)}, bf16[3,144,640]{2,1,0:T(8,128)(2,1)}, u32[]{:S(2)}, u32[]{:S(2)}) collective-permute-start(bf16[3,144,640]{2,1,0:T(8,128)(2,1)S(1)} %collective-permute-done.6.refs_3_.refs_10_.refs_9_), channel_id=1, source_target_pairs={{0,8},{8,0},{16,24},{24,16},{1,9},{9,1},{17,25},{25,17},{2,10},{10... | collective-permute-start | bytes 1658888 | tf_op jit(solution)/shard_map/ppermute | solution.py:285
  60.2 14.8 %collective-permute-start.8 = (bf16[3,144,640]{2,1,0:T(8,128)(2,1)S(1)}, bf16[3,144,640]{2,1,0:T(8,128)(2,1)S(1)}, u32[]{:S(2)}, u32[]{:S(2)}) collective-permute-start(bf16[3,144,640]{2,1,0:T(8,128)(2,1)S(1)} %collective-permute-done.6.refs_3_.refs_10_.refs_9_), channel_id=1, source_target_pairs={{0,16},{8,24},{16,0},{24,8},{1,17},{9,25},{17,1},{25,9},{2,18},{10... | collective-permute-start | bytes 1658888 | tf_op jit(solution)/shard_map/ppermute | solution.py:285
  82.8 4.0 %collective-permute-start.18 = (f32[16,640]{1,0:T(8,128)S(1)}, f32[16,640]{1,0:T(8,128)S(1)}, u32[]{:S(2)}, u32[]{:S(2)}) collective-permute-start(f32[16,640]{1,0:T(8,128)S(1)} %add.18), channel_id=1, source_target_pairs={{0,16},{8,24},{16,0},{24,8},{1,17},{9,25},{17,1},{25,9},{2,18},{10... | collective-permute-start | bytes 122888 | tf_op jit(solution)/shard_map/ppermute | solution.py:285
  86.8 4.5 %collective-permute-start.19 = (f32[16,640]{1,0:T(8,128)S(1)}, f32[16,640]{1,0:T(8,128)S(1)}, u32[]{:S(2)}, u32[]{:S(2)}) collective-permute-start(f32[16,640]{1,0:T(8,128)S(1)} %add.19), channel_id=1, source_target_pairs={{0,1},{1,0},{2,3},{3,2},{4,5},{5,4},{6,7},{7,6},{8,9},{9,8},{10,11... | collective-permute-start | bytes 122888 | tf_op jit(solution)/shard_map/ppermute | solution.py:285
  91.3 4.0 %collective-permute-start.20 = (f32[16,640]{1,0:T(8,128)S(1)}, f32[16,640]{1,0:T(8,128)S(1)}, u32[]{:S(2)}, u32[]{:S(2)}) collective-permute-start(f32[16,640]{1,0:T(8,128)S(1)} %add.20), channel_id=1, source_target_pairs={{0,2},{1,3},{2,0},{3,1},{4,6},{5,7},{6,4},{7,5},{8,10},{9,11},{10,... | collective-permute-start | bytes 122888 | tf_op jit(solution)/shard_map/ppermute | solution.py:285
  95.3 5.9 %collective-permute-start.21 = (f32[16,640]{1,0:T(8,128)S(1)}, f32[16,640]{1,0:T(8,128)S(1)}, u32[]{:S(2)}, u32[]{:S(2)}) collective-permute-start(f32[16,640]{1,0:T(8,128)S(1)} %add.21), channel_id=1, source_target_pairs={{0,4},{1,5},{2,6},{3,7},{4,0},{5,1},{6,2},{7,3},{8,12},{9,13},{10,... | collective-permute-start | bytes 122888 | tf_op jit(solution)/shard_map/ppermute | solution.py:285
  112.7 7.9 %collective-permute-start.24 = (bf16[208,512]{1,0:T(8,128)(2,1)}, bf16[208,512]{1,0:T(8,128)(2,1)S(1)}, u32[]{:S(2)}, u32[]{:S(2)}) collective-permute-start(bf16[208,512]{1,0:T(8,128)(2,1)} %get-tuple-element.154), channel_id=1, source_target_pairs={{0,1},{1,0},{2,3},{3,2},{4,5},{5,4},{6,7},{7,6},{8,9},{9,8},{10,11... | collective-permute-start | bytes 638984 | tf_op jit(solution)/shard_map/ppermute | solution.py:285
  113.8 9.9 %collective-permute-start.25 = (bf16[208,512]{1,0:T(8,128)(2,1)}, bf16[208,512]{1,0:T(8,128)(2,1)S(1)}, u32[]{:S(2)}, u32[]{:S(2)}) collective-permute-start(bf16[208,512]{1,0:T(8,128)(2,1)} %get-tuple-element.155), channel_id=1, source_target_pairs={{0,2},{1,3},{2,0},{3,1},{4,6},{5,7},{6,4},{7,5},{8,10},{9,11},{10,... | collective-permute-start | bytes 638984 | tf_op jit(solution)/shard_map/ppermute | solution.py:285
  114.0 17.6 %collective-permute-start.26 = (bf16[208,512]{1,0:T(8,128)(2,1)}, bf16[208,512]{1,0:T(8,128)(2,1)S(1)}, u32[]{:S(2)}, u32[]{:S(2)}) collective-permute-start(bf16[208,512]{1,0:T(8,128)(2,1)} %get-tuple-element.156), channel_id=1, source_target_pairs={{0,4},{1,5},{2,6},{3,7},{4,0},{5,1},{6,2},{7,3},{8,12},{9,13},{10,... | collective-permute-start | bytes 638984 | tf_op jit(solution)/shard_map/ppermute | solution.py:285
  116.9 24.8 %collective-permute-start.27 = (bf16[208,512]{1,0:T(8,128)(2,1)}, bf16[208,512]{1,0:T(8,128)(2,1)S(1)}, u32[]{:S(2)}, u32[]{:S(2)}) collective-permute-start(bf16[208,512]{1,0:T(8,128)(2,1)} %get-tuple-element.157), channel_id=1, source_target_pairs={{0,5},{1,4},{2,7},{3,6},{4,1},{5,0},{6,3},{7,2},{8,13},{9,12},{10,... | collective-permute-start | bytes 638984 | tf_op jit(solution)/shard_map/ppermute | solution.py:285
  118.2 23.5 %collective-permute-start.28 = (bf16[208,512]{1,0:T(8,128)(2,1)}, bf16[208,512]{1,0:T(8,128)(2,1)S(1)}, u32[]{:S(2)}, u32[]{:S(2)}) collective-permute-start(bf16[208,512]{1,0:T(8,128)(2,1)} %get-tuple-element.158), channel_id=1, source_target_pairs={{0,3},{1,2},{2,1},{3,0},{4,7},{5,6},{6,5},{7,4},{8,11},{9,10},{10,... | collective-permute-start | bytes 638984 | tf_op jit(solution)/shard_map/ppermute | solution.py:285
  120.6 26.8 %collective-permute-start.22 = (bf16[208,512]{1,0:T(8,128)(2,1)}, bf16[208,512]{1,0:T(8,128)(2,1)S(1)}, u32[]{:S(2)}, u32[]{:S(2)}) collective-permute-start(bf16[208,512]{1,0:T(8,128)(2,1)} %get-tuple-element.151), channel_id=1, source_target_pairs={{0,6},{1,7},{2,4},{3,5},{4,2},{5,3},{6,0},{7,1},{8,14},{9,15},{10,... | collective-permute-start | bytes 638984 | tf_op jit(solution)/shard_map/ppermute | solution.py:285
  123.7 26.9 %collective-permute-start.23 = (bf16[208,512]{1,0:T(8,128)(2,1)}, bf16[208,512]{1,0:T(8,128)(2,1)S(1)}, u32[]{:S(2)}, u32[]{:S(2)}) collective-permute-start(bf16[208,512]{1,0:T(8,128)(2,1)} %get-tuple-element.152), channel_id=1, source_target_pairs={{0,7},{1,6},{2,5},{3,4},{4,3},{5,2},{6,1},{7,0},{8,15},{9,14},{10,... | collective-permute-start | bytes 638984 | tf_op jit(solution)/shard_map/ppermute | solution.py:285
  (13 other events, 97.6 us)

commit v4 on v3

--- a/solution.py
+++ b/solution.py
@@ -437,7 +437,7 @@
             in_specs=[smem, smem, smem, vmem] + places + [anywhere] * len(arrays),
             out_specs=vmem if first else [vmem, vmem],
             scratch_shapes=[pltpu.VMEM(held.shape, held.dtype)] * first + room,
-            compiler_params=params,
+            compiler_params=pltpu.CompilerParams(vmem_limit_bytes=big_vmem // 2),
             cost_estimate=pl.CostEstimate(
                 flops=2 * tile_count * len(keys) // len(every) * slots * width * points,
                 bytes_accessed=1 << 27,

time: 153 us -> 153 us (level)
  no operation moved by 1% of the time
where the time goes in v4:
time: 153 us; the launch traced here: 152 us
  waiting for transfers between devices  68.1 us (45%)
  starting transfers between devices  42.6 us (28%)
  Pallas kernels  35 us (23%)
  local copies, waits for them, and re-layouts  4.23 us (3%)
    ppermute x29, waiting for transfers between devices, swap(): return lax.ppermute(value, axis, [(i, i ^ offset) for i in range(size)])  68.1 us
    ppermute x29, starting transfers between devices, swap(): return lax.ppermute(value, axis, [(i, i ^ offset) for i in range(size)])  35.9 us
    pallas_call x2, Pallas kernels, forward(): pl.pallas_call(functools.partial(forward_kernel, plan, piece, 1.0 / all_b...  12.6 us
    pallas_call x1, Pallas kernels, body(): pl.pallas_call(functools.partial(backward_kernel, n, count, tiles_dev, pi...  10.8 us
    all_to_all x1, starting transfers between devices, across(): lax.all_to_all(value, 'grid', split_axis=0, concat_axis=0, tiled=True)  6.7 us
    pallas_call x2, Pallas kernels, body(): pl.pallas_call(functools.partial(unpack_kernel, groups, per, tuple(offset...  4.16 us
    pallas_call x1, Pallas kernels, body(): pl.pallas_call(functools.partial(pack_kernel, groups, per), out_shape=[ja...  3.55 us
  transfers between devices with their start and end apart: 30, of which 19 were waited for; matrix products, arithmetic and copies ran while one was open for 1% of the time, Pallas kernels for 11%

profile of v4, /device:TPU:8, one launch (start us, length us, event | category | flops | bytes accessed | tf_op | source)
XLA Modules:
  0.0 152.5 jit_solution(18335707197231103428)
XLA Ops:
  8.0 3.5 %pack.1 = (bf16[8,208,512]{2,1,0:T(8,128)(2,1)}, bf16[8,48,512]{2,1,0:T(8,128)(2,1)}) custom-call(s32[16]{0:T(128)} %rows_ref.5, bf16[16,16,3840]{2,1,0:T(8,128)(2,1)} %coef_ref.1), custom_call_target="tpu_custom_call" | custom-call | tf_op jit(solution)/shard_map/pack/pallas_call | solution.py:350
  11.6 7.4 %collective-permute-done.2 = bf16[144,640]{1,0:T(8,128)(2,1)S(1)} collective-permute-done((bf16[144,640]{1,0:T(8,128)(2,1)S(1)}, bf16[144,640]{1,0:T(8,128)(2,1)S(1)}, u32[]{:S(2)}, u32[]{:S(2)}) %collective-permute-start.2) | collective-permute-done | bytes 184352 | tf_op jit(solution)/shard_map/ppermute | solution.py:285
  19.0 2.0 %collective-permute-done.1 = bf16[144,640]{1,0:T(8,128)(2,1)S(1)} collective-permute-done((bf16[144,640]{1,0:T(8,128)(2,1)S(1)}, bf16[144,640]{1,0:T(8,128)(2,1)S(1)}, u32[]{:S(2)}, u32[]{:S(2)}) %collective-permute-start.1) | collective-permute-done | bytes 184352 | tf_op jit(solution)/shard_map/ppermute | solution.py:285
  21.0 6.7 %all-to-all-start.2 = ((bf16[8,208,512]{2,1,0:T(8,128)(2,1)}), bf16[8,208,512]{2,1,0:T(8,128)(2,1)}, u32[]{:S(2)}, u32[]{:S(2)}) async-start(bf16[8,208,512]{2,1,0:T(8,128)(2,1)} %get-tuple-element.138), calls=%async_computation.2 | async-start | bytes 3407872 | tf_op jit(solution)/shard_map/all_to_all | solution.py:320
  34.8 13.5 %collective-permute-done.4.refs_5_.refs_4_ = bf16[1,144,640]{2,1,0:T(8,128)(2,1)S(1)} collective-permute-done((bf16[1,144,640]{2,1,0:T(8,128)(2,1)S(1)}, bf16[1,144,640]{2,1,0:T(8,128)(2,1)S(1)}, u32[]{:S(2)}, u32[]{:S(2)}) %collective-permute-start.4) | collective-permute-done | bytes 184352 | tf_op jit(solution)/shard_map/ppermute | solution.py:285
  48.2 2.0 %collective-permute-done.7.refs_2_.refs_12_ = bf16[1,144,640]{2,1,0:T(8,128)(2,1)S(1)} collective-permute-done((bf16[1,144,640]{2,1,0:T(8,128)(2,1)S(1)}, bf16[1,144,640]{2,1,0:T(8,128)(2,1)S(1)}, u32[]{:S(2)}, u32[]{:S(2)}) %collective-permute-start.7) | collective-permute-done | bytes 184352 | tf_op jit(solution)/shard_map/ppermute | solution.py:285
  50.2 7.0 %collective-permute-done.6.refs_3_.refs_10_.refs_9_ = bf16[3,144,640]{2,1,0:T(8,128)(2,1)S(1)} collective-permute-done((bf16[3,144,640]{2,1,0:T(8,128)(2,1)S(1)}, bf16[3,144,640]{2,1,0:T(8,128)(2,1)S(1)}, u32[]{:S(2)}, u32[]{:S(2)}) %collective-permute-start.6) | collective-permute-done | bytes 552992 | tf_op jit(solution)/shard_map/ppermute | solution.py:285
  64.5 8.5 %forward.6 = (f32[16,640]{1,0:T(8,128)S(1)}, bf16[128,16,512]{2,1,0:T(8,128)(2,1)}) custom-call(s32[16,16]{1,0:T(8,128)S(1)} %get-tuple-element.133.touch_ref, s32[8,16]{1,0:T(8,128)S(1)} %get-tuple-element.134.rows_ref, s32[2]{0:T(128)S(1)} %pad_add_fusion.at_ref, f32[512,128]{1,0:T(8,128)S(1)} %get-tuple-element.137.weight_ref, ...), custom_call_target="tpu_custom_call" | custom-call | flops 2013265920 | bytes 134217728 | tf_op jit(solution)/shard_map/forward/pallas_call | solution.py:434
  77.2 4.0 %forward.7 = f32[16,640]{1,0:T(8,128)S(1)} custom-call(s32[16,16]{1,0:T(8,128)S(1)} %get-tuple-element.133.touch_ref, s32[8,16]{1,0:T(8,128)S(1)} %get-tuple-element.134.rows_ref, s32[2]{0:T(128)S(1)} %pad_add_fusion.at_ref, f32[512,128]{1,0:T(8,128)S(1)} %get-tuple-element.137.weight_ref, f32[16,640]{1,0:T(8,128)S(1)} %get-tuple-element.143.refs_0_, ...), custom_call_target="tpu_custom_call" | custom-call | flops 671088640 | bytes 134217728 | tf_op jit(solution)/shard_map/forward/pallas_call | solution.py:434
  84.2 2.5 %collective-permute-done.18 = f32[16,640]{1,0:T(8,128)S(1)} collective-permute-done((f32[16,640]{1,0:T(8,128)S(1)}, f32[16,640]{1,0:T(8,128)S(1)}, u32[]{:S(2)}, u32[]{:S(2)}) %collective-permute-start.18) | collective-permute-done | bytes 40992 | tf_op jit(solution)/shard_map/ppermute | solution.py:285
  86.7 2.5 %collective-permute-start.19 = (f32[16,640]{1,0:T(8,128)S(1)}, f32[16,640]{1,0:T(8,128)S(1)}, u32[]{:S(2)}, u32[]{:S(2)}) collective-permute-start(f32[16,640]{1,0:T(8,128)S(1)} %add.19), channel_id=1, source_target_pairs={{0,1},{1,0},{2,3},{3,2},{4,5},{5,4},{6,7},{7,6},{8,9},{9,8},{10,11... | collective-permute-start | bytes 122888 | tf_op jit(solution)/shard_map/ppermute | solution.py:285
  89.2 2.0 %collective-permute-done.19 = f32[16,640]{1,0:T(8,128)S(1)} collective-permute-done((f32[16,640]{1,0:T(8,128)S(1)}, f32[16,640]{1,0:T(8,128)S(1)}, u32[]{:S(2)}, u32[]{:S(2)}) %collective-permute-start.19) | collective-permute-done | bytes 40992 | tf_op jit(solution)/shard_map/ppermute | solution.py:285
  91.2 2.0 %collective-permute-start.20 = (f32[16,640]{1,0:T(8,128)S(1)}, f32[16,640]{1,0:T(8,128)S(1)}, u32[]{:S(2)}, u32[]{:S(2)}) collective-permute-start(f32[16,640]{1,0:T(8,128)S(1)} %add.20), channel_id=1, source_target_pairs={{0,2},{1,3},{2,0},{3,1},{4,6},{5,7},{6,4},{7,5},{8,10},{9,11},{10,... | collective-permute-start | bytes 122888 | tf_op jit(solution)/shard_map/ppermute | solution.py:285
  93.2 2.0 %collective-permute-done.20 = f32[16,640]{1,0:T(8,128)S(1)} collective-permute-done((f32[16,640]{1,0:T(8,128)S(1)}, f32[16,640]{1,0:T(8,128)S(1)}, u32[]{:S(2)}, u32[]{:S(2)}) %collective-permute-start.20) | collective-permute-done | bytes 40992 | tf_op jit(solution)/shard_map/ppermute | solution.py:285
  95.2 3.9 %collective-permute-start.21 = (f32[16,640]{1,0:T(8,128)S(1)}, f32[16,640]{1,0:T(8,128)S(1)}, u32[]{:S(2)}, u32[]{:S(2)}) collective-permute-start(f32[16,640]{1,0:T(8,128)S(1)} %add.21), channel_id=1, source_target_pairs={{0,4},{1,5},{2,6},{3,7},{4,0},{5,1},{6,2},{7,3},{8,12},{9,13},{10,... | collective-permute-start | bytes 122888 | tf_op jit(solution)/shard_map/ppermute | solution.py:285
  99.1 2.0 %collective-permute-done.21 = f32[16,640]{1,0:T(8,128)S(1)} collective-permute-done((f32[16,640]{1,0:T(8,128)S(1)}, f32[16,640]{1,0:T(8,128)S(1)}, u32[]{:S(2)}, u32[]{:S(2)}) %collective-permute-start.21) | collective-permute-done | bytes 40992 | tf_op jit(solution)/shard_map/ppermute | solution.py:285
  101.8 10.8 %backward.1 = (bf16[208,512]{1,0:T(8,128)(2,1)}, bf16[208,512]{1,0:T(8,128)(2,1)}, bf16[208,512]{1,0:T(8,128)(2,1)}, bf16[208,512]{1,0:T(8,128)(2,1)}, bf16[208,...) custom-call(s32[16,16]{1,0:T(8,128)S(1)} %get-tuple-element.133.touc, ...), custom_call_target="tpu_custom_call" | custom-call | tf_op jit(solution)/shard_map/backward/pallas_call | solution.py:474
  113.9 2.9 %collective-permute-start.26 = (bf16[208,512]{1,0:T(8,128)(2,1)}, bf16[208,512]{1,0:T(8,128)(2,1)S(1)}, u32[]{:S(2)}, u32[]{:S(2)}) collective-permute-start(bf16[208,512]{1,0:T(8,128)(2,1)} %get-tuple-element.156), channel_id=1, source_target_pairs={{0,4},{1,5},{2,6},{3,7},{4,0},{5,1},{6,2},{7,3},{8,12},{9,13},{10,... | collective-permute-start | bytes 638984 | tf_op jit(solution)/shard_map/ppermute | solution.py:285
  120.5 3.1 %collective-permute-start.22 = (bf16[208,512]{1,0:T(8,128)(2,1)}, bf16[208,512]{1,0:T(8,128)(2,1)S(1)}, u32[]{:S(2)}, u32[]{:S(2)}) collective-permute-start(bf16[208,512]{1,0:T(8,128)(2,1)} %get-tuple-element.151), channel_id=1, source_target_pairs={{0,6},{1,7},{2,4},{3,5},{4,2},{5,3},{6,0},{7,1},{8,14},{9,15},{10,... | collective-permute-start | bytes 638984 | tf_op jit(solution)/shard_map/ppermute | solution.py:285
  126.8 4.6 %collective-permute-done.26.refs_3_ = bf16[208,512]{1,0:T(8,128)(2,1)S(1)} collective-permute-done((bf16[208,512]{1,0:T(8,128)(2,1)}, bf16[208,512]{1,0:T(8,128)(2,1)S(1)}, u32[]{:S(2)}, u32[]{:S(2)}) %collective-permute-start.26) | collective-permute-done | bytes 213024 | tf_op jit(solution)/shard_map/ppermute | solution.py:285
  131.5 10.1 %collective-permute-done.27.refs_4_ = bf16[208,512]{1,0:T(8,128)(2,1)S(1)} collective-permute-done((bf16[208,512]{1,0:T(8,128)(2,1)}, bf16[208,512]{1,0:T(8,128)(2,1)S(1)}, u32[]{:S(2)}, u32[]{:S(2)}) %collective-permute-start.27) | collective-permute-done | bytes 213024 | tf_op jit(solution)/shard_map/ppermute | solution.py:285
  142.6 2.4 %unpack.2.refs_2_ = f32[16,16,3840]{2,1,0:T(8,128)} custom-call(s32[16]{0:T(128)S(1)} %copy-done.1, s32[2]{0:T(128)S(1)} %pad_add_fusion.at_ref, bf16[8,48,512]{2,1,0:T(8,128)(2,1)S(1)} %get-tuple-element.166.spill_ref, bf16[208,512]{1,0:T(8,128)(2,1)S(1)} %copy-done, bf16[208,512]{1,0:T(8,128)(2,1)S(1)} %collective-permute-done.24.refs_1_, ...), custom_call_target="tpu_custom_call" | custom-call | bytes 4194304 | tf_op jit(solution)/shard_map/unpack/pallas_call | solution.py:491
  145.0 2.3 %collective-permute-done.22.refs_0_ = bf16[208,512]{1,0:T(8,128)(2,1)S(1)} collective-permute-done((bf16[208,512]{1,0:T(8,128)(2,1)}, bf16[208,512]{1,0:T(8,128)(2,1)S(1)}, u32[]{:S(2)}, u32[]{:S(2)}) %collective-permute-start.22) | collective-permute-done | bytes 213024 | tf_op jit(solution)/shard_map/ppermute | solution.py:285
  147.3 3.2 %collective-permute-done.23.refs_1_ = bf16[208,512]{1,0:T(8,128)(2,1)S(1)} collective-permute-done((bf16[208,512]{1,0:T(8,128)(2,1)}, bf16[208,512]{1,0:T(8,128)(2,1)S(1)}, u32[]{:S(2)}, u32[]{:S(2)}) %collective-permute-start.23) | collective-permute-done | bytes 213024 | tf_op jit(solution)/shard_map/ppermute | solution.py:285
  (70 shorter events, 39.8 us)
Async XLA Ops:
  2.4 9.2 %collective-permute-start.3 = (bf16[1,144,640]{2,1,0:T(8,128)(2,1)S(1)}, bf16[1,144,640]{2,1,0:T(8,128)(2,1)S(1)}, u32[]{:S(2)}, u32[]{:S(2)}) collective-permute-start(bf16[1,144,640]{2,1,0:T(8,128)(2,1)S(1)} %bitcast.10), channel_id=1, source_target_pairs={{0,1},{1,0},{2,3},{3,2},{4,5},{5,4},{6,7},{7,6},{8,9},{9,8},{10,11... | collective-permute-start | bytes 552968 | tf_op jit(solution)/shard_map/ppermute | solution.py:285
  4.0 15.0 %collective-permute-start.2 = (bf16[144,640]{1,0:T(8,128)(2,1)S(1)}, bf16[144,640]{1,0:T(8,128)(2,1)S(1)}, u32[]{:S(2)}, u32[]{:S(2)}) collective-permute-start(bf16[144,640]{1,0:T(8,128)(2,1)S(1)} %prep.1), channel_id=1, source_target_pairs={{0,6},{1,7},{2,4},{3,5},{4,2},{5,3},{6,0},{7,1},{8,14},{9,15},{10,... | collective-permute-start | bytes 552968 | tf_op jit(solution)/shard_map/ppermute | solution.py:285
  5.5 15.5 %collective-permute-start.1 = (bf16[144,640]{1,0:T(8,128)(2,1)S(1)}, bf16[144,640]{1,0:T(8,128)(2,1)S(1)}, u32[]{:S(2)}, u32[]{:S(2)}) collective-permute-start(bf16[144,640]{1,0:T(8,128)(2,1)S(1)} %prep.1), channel_id=1, source_target_pairs={{0,4},{1,5},{2,6},{3,7},{4,0},{5,1},{6,2},{7,3},{8,12},{9,13},{10,... | collective-permute-start | bytes 552968 | tf_op jit(solution)/shard_map/ppermute | solution.py:285
  6.8 14.2 %collective-permute-start = (bf16[144,640]{1,0:T(8,128)(2,1)S(1)}, bf16[144,640]{1,0:T(8,128)(2,1)S(1)}, u32[]{:S(2)}, u32[]{:S(2)}) collective-permute-start(bf16[144,640]{1,0:T(8,128)(2,1)S(1)} %prep.1), channel_id=1, source_target_pairs={{0,2},{1,3},{2,0},{3,1},{4,6},{5,7},{6,4},{7,5},{8,10},{9,11},{10,... | collective-permute-start | bytes 552968 | tf_op jit(solution)/shard_map/ppermute | solution.py:285
  21.0 43.5 %all-to-all-start.2 = ((bf16[8,208,512]{2,1,0:T(8,128)(2,1)}), bf16[8,208,512]{2,1,0:T(8,128)(2,1)}, u32[]{:S(2)}, u32[]{:S(2)}) async-start(bf16[8,208,512]{2,1,0:T(8,128)(2,1)} %get-tuple-element.138), calls=%async_computation.2 | async-start | bytes 3407872 | tf_op jit(solution)/shard_map/all_to_all | solution.py:320
  27.8 29.5 %collective-permute-start.6 = (bf16[3,144,640]{2,1,0:T(8,128)(2,1)S(1)}, bf16[3,144,640]{2,1,0:T(8,128)(2,1)S(1)}, u32[]{:S(2)}, u32[]{:S(2)}) collective-permute-start(bf16[3,144,640]{2,1,0:T(8,128)(2,1)S(1)} %pad_maximum_fusion.after_ref.refs_1_.refs_2_), channel_id=1, source_target_pairs={{0,1},{1,0},{2,3},{3,2},{4,5},{5,4},{6,7},{7,6},{8,9},{9,8},{10,11... | collective-permute-start | bytes 1658888 | tf_op jit(solution)/shard_map/ppermute | solution.py:285
  29.3 27.9 %collective-permute-start.5 = (bf16[3,144,640]{2,1,0:T(8,128)(2,1)S(1)}, bf16[3,144,640]{2,1,0:T(8,128)(2,1)S(1)}, u32[]{:S(2)}, u32[]{:S(2)}) collective-permute-start(bf16[3,144,640]{2,1,0:T(8,128)(2,1)S(1)} %pad_maximum_fusion.after_ref.refs_1_.refs_2_), channel_id=1, source_target_pairs={{0,16},{8,24},{16,0},{24,8},{1,17},{9,25},{17,1},{25,9},{2,18},{10... | collective-permute-start | bytes 1658888 | tf_op jit(solution)/shard_map/ppermute | solution.py:285
  30.8 17.4 %collective-permute-start.4 = (bf16[1,144,640]{2,1,0:T(8,128)(2,1)S(1)}, bf16[1,144,640]{2,1,0:T(8,128)(2,1)S(1)}, u32[]{:S(2)}, u32[]{:S(2)}) collective-permute-start(bf16[1,144,640]{2,1,0:T(8,128)(2,1)S(1)} %bitcast.11), channel_id=1, source_target_pairs={{0,16},{8,24},{16,0},{24,8},{1,17},{9,25},{17,1},{25,9},{2,18},{10... | collective-permute-start | bytes 552968 | tf_op jit(solution)/shard_map/ppermute | solution.py:285
  31.3 18.9 %collective-permute-start.7 = (bf16[1,144,640]{2,1,0:T(8,128)(2,1)S(1)}, bf16[1,144,640]{2,1,0:T(8,128)(2,1)S(1)}, u32[]{:S(2)}, u32[]{:S(2)}) collective-permute-start(bf16[1,144,640]{2,1,0:T(8,128)(2,1)S(1)} %collective-permute-done.3.refs_2_.refs_9_.refs_8_), channel_id=1, source_target_pairs={{0,16},{8,24},{16,0},{24,8},{1,17},{9,25},{17,1},{25,9},{2,18},{10... | collective-permute-start | bytes 552968 | tf_op jit(solution)/shard_map/ppermute | solution.py:285
  57.3 6.5 %collective-permute-start.12 = (bf16[3,144,640]{2,1,0:T(8,128)(2,1)S(1)}, bf16[3,144,640]{2,1,0:T(8,128)(2,1)}, u32[]{:S(2)}, u32[]{:S(2)}) collective-permute-start(bf16[3,144,640]{2,1,0:T(8,128)(2,1)S(1)} %collective-permute-done.5.refs_6_.refs_5_), channel_id=1, source_target_pairs={{0,8},{8,0},{16,24},{24,16},{1,9},{9,1},{17,25},{25,17},{2,10},{10... | collective-permute-start | bytes 1658888 | tf_op jit(solution)/shard_map/ppermute | solution.py:285
  57.3 6.5 %collective-permute-start.10 = (bf16[3,144,640]{2,1,0:T(8,128)(2,1)S(1)}, bf16[3,144,640]{2,1,0:T(8,128)(2,1)}, u32[]{:S(2)}, u32[]{:S(2)}) collective-permute-start(bf16[3,144,640]{2,1,0:T(8,128)(2,1)S(1)} %pad_maximum_fusion.after_ref.refs_1_.refs_2_), channel_id=1, source_target_pairs={{0,8},{8,0},{16,24},{24,16},{1,9},{9,1},{17,25},{25,17},{2,10},{10... | collective-permute-start | bytes 1658888 | tf_op jit(solution)/shard_map/ppermute | solution.py:285
  57.8 6.7 %collective-permute-start.14 = (bf16[3,144,640]{2,1,0:T(8,128)(2,1)S(1)}, bf16[3,144,640]{2,1,0:T(8,128)(2,1)}, u32[]{:S(2)}, u32[]{:S(2)}) collective-permute-start(bf16[3,144,640]{2,1,0:T(8,128)(2,1)S(1)} %collective-permute-done.6.refs_3_.refs_10_.refs_9_), channel_id=1, source_target_pairs={{0,8},{8,0},{16,24},{24,16},{1,9},{9,1},{17,25},{25,17},{2,10},{10... | collective-permute-start | bytes 1658888 | tf_op jit(solution)/shard_map/ppermute | solution.py:285
  60.2 14.8 %collective-permute-start.8 = (bf16[3,144,640]{2,1,0:T(8,128)(2,1)S(1)}, bf16[3,144,640]{2,1,0:T(8,128)(2,1)S(1)}, u32[]{:S(2)}, u32[]{:S(2)}) collective-permute-start(bf16[3,144,640]{2,1,0:T(8,128)(2,1)S(1)} %collective-permute-done.6.refs_3_.refs_10_.refs_9_), channel_id=1, source_target_pairs={{0,16},{8,24},{16,0},{24,8},{1,17},{9,25},{17,1},{25,9},{2,18},{10... | collective-permute-start | bytes 1658888 | tf_op jit(solution)/shard_map/ppermute | solution.py:285
  82.7 4.0 %collective-permute-start.18 = (f32[16,640]{1,0:T(8,128)S(1)}, f32[16,640]{1,0:T(8,128)S(1)}, u32[]{:S(2)}, u32[]{:S(2)}) collective-permute-start(f32[16,640]{1,0:T(8,128)S(1)} %add.18), channel_id=1, source_target_pairs={{0,16},{8,24},{16,0},{24,8},{1,17},{9,25},{17,1},{25,9},{2,18},{10... | collective-permute-start | bytes 122888 | tf_op jit(solution)/shard_map/ppermute | solution.py:285
  86.7 4.5 %collective-permute-start.19 = (f32[16,640]{1,0:T(8,128)S(1)}, f32[16,640]{1,0:T(8,128)S(1)}, u32[]{:S(2)}, u32[]{:S(2)}) collective-permute-start(f32[16,640]{1,0:T(8,128)S(1)} %add.19), channel_id=1, source_target_pairs={{0,1},{1,0},{2,3},{3,2},{4,5},{5,4},{6,7},{7,6},{8,9},{9,8},{10,11... | collective-permute-start | bytes 122888 | tf_op jit(solution)/shard_map/ppermute | solution.py:285
  91.2 4.0 %collective-permute-start.20 = (f32[16,640]{1,0:T(8,128)S(1)}, f32[16,640]{1,0:T(8,128)S(1)}, u32[]{:S(2)}, u32[]{:S(2)}) collective-permute-start(f32[16,640]{1,0:T(8,128)S(1)} %add.20), channel_id=1, source_target_pairs={{0,2},{1,3},{2,0},{3,1},{4,6},{5,7},{6,4},{7,5},{8,10},{9,11},{10,... | collective-permute-start | bytes 122888 | tf_op jit(solution)/shard_map/ppermute | solution.py:285
  95.2 5.9 %collective-permute-start.21 = (f32[16,640]{1,0:T(8,128)S(1)}, f32[16,640]{1,0:T(8,128)S(1)}, u32[]{:S(2)}, u32[]{:S(2)}) collective-permute-start(f32[16,640]{1,0:T(8,128)S(1)} %add.21), channel_id=1, source_target_pairs={{0,4},{1,5},{2,6},{3,7},{4,0},{5,1},{6,2},{7,3},{8,12},{9,13},{10,... | collective-permute-start | bytes 122888 | tf_op jit(solution)/shard_map/ppermute | solution.py:285
  112.6 7.9 %collective-permute-start.24 = (bf16[208,512]{1,0:T(8,128)(2,1)}, bf16[208,512]{1,0:T(8,128)(2,1)S(1)}, u32[]{:S(2)}, u32[]{:S(2)}) collective-permute-start(bf16[208,512]{1,0:T(8,128)(2,1)} %get-tuple-element.154), channel_id=1, source_target_pairs={{0,1},{1,0},{2,3},{3,2},{4,5},{5,4},{6,7},{7,6},{8,9},{9,8},{10,11... | collective-permute-start | bytes 638984 | tf_op jit(solution)/shard_map/ppermute | solution.py:285
  113.7 9.9 %collective-permute-start.25 = (bf16[208,512]{1,0:T(8,128)(2,1)}, bf16[208,512]{1,0:T(8,128)(2,1)S(1)}, u32[]{:S(2)}, u32[]{:S(2)}) collective-permute-start(bf16[208,512]{1,0:T(8,128)(2,1)} %get-tuple-element.155), channel_id=1, source_target_pairs={{0,2},{1,3},{2,0},{3,1},{4,6},{5,7},{6,4},{7,5},{8,10},{9,11},{10,... | collective-permute-start | bytes 638984 | tf_op jit(solution)/shard_map/ppermute | solution.py:285
  113.9 17.6 %collective-permute-start.26 = (bf16[208,512]{1,0:T(8,128)(2,1)}, bf16[208,512]{1,0:T(8,128)(2,1)S(1)}, u32[]{:S(2)}, u32[]{:S(2)}) collective-permute-start(bf16[208,512]{1,0:T(8,128)(2,1)} %get-tuple-element.156), channel_id=1, source_target_pairs={{0,4},{1,5},{2,6},{3,7},{4,0},{5,1},{6,2},{7,3},{8,12},{9,13},{10,... | collective-permute-start | bytes 638984 | tf_op jit(solution)/shard_map/ppermute | solution.py:285
  116.8 24.8 %collective-permute-start.27 = (bf16[208,512]{1,0:T(8,128)(2,1)}, bf16[208,512]{1,0:T(8,128)(2,1)S(1)}, u32[]{:S(2)}, u32[]{:S(2)}) collective-permute-start(bf16[208,512]{1,0:T(8,128)(2,1)} %get-tuple-element.157), channel_id=1, source_target_pairs={{0,5},{1,4},{2,7},{3,6},{4,1},{5,0},{6,3},{7,2},{8,13},{9,12},{10,... | collective-permute-start | bytes 638984 | tf_op jit(solution)/shard_map/ppermute | solution.py:285
  118.1 23.5 %collective-permute-start.28 = (bf16[208,512]{1,0:T(8,128)(2,1)}, bf16[208,512]{1,0:T(8,128)(2,1)S(1)}, u32[]{:S(2)}, u32[]{:S(2)}) collective-permute-start(bf16[208,512]{1,0:T(8,128)(2,1)} %get-tuple-element.158), channel_id=1, source_target_pairs={{0,3},{1,2},{2,1},{3,0},{4,7},{5,6},{6,5},{7,4},{8,11},{9,10},{10,... | collective-permute-start | bytes 638984 | tf_op jit(solution)/shard_map/ppermute | solution.py:285
  120.5 26.8 %collective-permute-start.22 = (bf16[208,512]{1,0:T(8,128)(2,1)}, bf16[208,512]{1,0:T(8,128)(2,1)S(1)}, u32[]{:S(2)}, u32[]{:S(2)}) collective-permute-start(bf16[208,512]{1,0:T(8,128)(2,1)} %get-tuple-element.151), channel_id=1, source_target_pairs={{0,6},{1,7},{2,4},{3,5},{4,2},{5,3},{6,0},{7,1},{8,14},{9,15},{10,... | collective-permute-start | bytes 638984 | tf_op jit(solution)/shard_map/ppermute | solution.py:285
  123.6 27.0 %collective-permute-start.23 = (bf16[208,512]{1,0:T(8,128)(2,1)}, bf16[208,512]{1,0:T(8,128)(2,1)S(1)}, u32[]{:S(2)}, u32[]{:S(2)}) collective-permute-start(bf16[208,512]{1,0:T(8,128)(2,1)} %get-tuple-element.152), channel_id=1, source_target_pairs={{0,7},{1,6},{2,5},{3,4},{4,3},{5,2},{6,1},{7,0},{8,15},{9,14},{10,... | collective-permute-start | bytes 638984 | tf_op jit(solution)/shard_map/ppermute | solution.py:285
  (13 other events, 97.4 us)
